TPU v7x, 32 devices: a whole 2x2x4 slice. The times are simulated.
32 devices in a mesh: group: 2 (over y), ctx: 8 (over z, core), head: 2 (over x).
Axes of the slice: x: 2, y: 2, z: 4, core: 2. Of those that a mesh axis runs over, the one named last changes fastest.
Arguments:
- queries: bfloat16 [2048, 4096], P(('group', 'ctx'), 'head'), parts along dimension 0, may hold values from -6 to 6
- keys: bfloat16 [2048, 512], P(('group', 'ctx'), 'head'), parts along dimension 0, may hold values from -6 to 6
- values: bfloat16 [2048, 512], P(('group', 'ctx'), 'head'), parts along dimension 0, may hold values from -6 to 6
- sinks: float32 [64], P('head'), may hold values from 0 to 4
- segments: int32 [2048], P('group'), parts along dimension 0, may hold values from 0 to 3, never falling along the last dimension, each value on 1 to 768 neighbouring positions
- hidden_in: bfloat16 [2048, 2880], P(('group', 'ctx')), parts along dimension 0, may hold values from -6 to 6
- routes: int32 [2048, 4], P(('group', 'ctx')), parts along dimension 0, may hold values from 0 to 7, all different within a row; in each aligned block of 64 rows (0 to 63, 64 to 127, ...) at most 48 rows name the same one
- w_out: bfloat16 [4096, 2880], P('head'), may hold values from -0.09375 to 0.09375
- norm_gain: float32 [2880], replicated, may hold values from 0.1 to 1.9
- router: bfloat16 [2880, 8], replicated, may hold values from -0.109375 to 0.109375
- w_gate_up: bfloat16 [8, 2, 2880, 2880], P('ctx', None, None, 'head'), may hold values from -0.109375 to 0.109375
- w_down: bfloat16 [8, 2880, 2880], P('ctx', 'head'), may hold values from -0.109375 to 0.109375
Outputs:
- layer_out: bfloat16 [2048, 2880], P(('group', 'ctx', 'head')), parts along dimension 0
There are 2 independent parts, one for each index of `group`. A program takes and returns all parts, laid end to end along the dimension named above; an argument that names none is the same for every part. Nothing has to cross between parts.
Inputs may be any that keep to these rules, and one draw needn't show every extreme that they name: `routes`: each row names 4 different experts; in each aligned block of 64 rows no expert is named by more than 48 rows, a bound that some block reaches. `segments`: requests fill consecutive positions in order; the longest has 768 positions.
All inputs are finite; a program needn't handle non-finite values.
Results may differ from a plain program's by a relative error of at most 0.015.
Values may be sent and summed in bfloat16 or wider, within the bound.
A program may use at most 128 MiB of HBM per device.

v0:
```python
import functools

import jax
import jax.numpy as jnp
from jax import lax
from jax.experimental import pallas as pl
from jax.experimental.pallas import tpu as pltpu
from jax.sharding import PartitionSpec as P

HEAD_SIZE = 64


masked_value = -1e30


def attend_kernel(
    query_ref, key_ref, value_ref, sink_ref, place_ref, segment_ref, own_segment_ref, out_ref
):
    rows = query_ref.shape[0]
    kv_groups = key_ref.shape[1] // HEAD_SIZE
    share = query_ref.shape[1] // key_ref.shape[1]
    spot = lax.broadcasted_iota(jnp.int32, (rows, key_ref.shape[0]), 1)
    visible = (spot <= place_ref[...]) & (segment_ref[...] == own_segment_ref[...])
    hidden_bias = jnp.where(visible, 0.0, masked_value)
    for group in range(kv_groups):
        span = slice(group * HEAD_SIZE, (group + 1) * HEAD_SIZE)
        group_keys = key_ref[:, span]
        group_values = value_ref[:, span]
        for pair in range(share // 2):
            both = []
            for member in range(2):
                head = group * share + pair * 2 + member
                query = query_ref[:, head * HEAD_SIZE : (head + 1) * HEAD_SIZE]
                scores = lax.dot_general(
                    query, group_keys, (((1,), (1,)), ((), ())), preferred_element_type=jnp.float32
                )
                scores = scores * HEAD_SIZE ** (-0.5) + hidden_bias
                sink = sink_ref[:, head : head + 1]
                top = jnp.maximum(jnp.max(scores, axis=-1, keepdims=True), sink)
                weights = jnp.exp(scores - top)
                total = jnp.sum(weights, axis=-1, keepdims=True) + jnp.exp(sink - top)
                mixed = jnp.dot(weights.astype(jnp.bfloat16), group_values, preferred_element_type=jnp.float32)
                both.append((mixed / total).astype(jnp.bfloat16))
            first = (group * share + pair * 2) * HEAD_SIZE
            out_ref[:, first : first + 2 * HEAD_SIZE] = jnp.concatenate(both, axis=1)


def attend(queries, all_keys, all_values, sinks, tok_pos, tok_seg, segments):
    return pl.pallas_call(
        attend_kernel,
        out_shape=jax.ShapeDtypeStruct(queries.shape, jnp.bfloat16),
        in_specs=[full_vmem()] * 7,
        out_specs=full_vmem(),
        name="attend",
    )(
        queries,
        all_keys,
        all_values,
        sinks.reshape(1, -1),
        tok_pos.reshape(-1, 1),
        segments.reshape(1, -1),
        tok_seg.reshape(-1, 1),
    )


MESH = pl.DeviceIdType.MESH
LANES = 128
CORES = 2


def full_vmem():
    return pl.BlockSpec(memory_space=pltpu.VMEM)


class Ring:
    def __init__(self, chips, heads):
        self.chips, self.heads, self.count = chips, heads, chips * heads
        ctx = lax.axis_index("ctx")
        self.head = lax.axis_index("head")
        self.core = lax.rem(ctx, CORES)
        z = lax.div(ctx, CORES)
        self.place = self.head * chips + z + lax.rem(self.head, 2) * (chips - 1 - 2 * z)
        self.partner = {"ctx": z * CORES + 1 - self.core, "head": self.head}

    def at(self, offset):
        spot = lax.rem(self.place + offset + self.count, self.count)
        head = lax.div(spot, self.chips)
        step = lax.rem(spot, self.chips)
        return head, step + lax.rem(head, 2) * (self.chips - 1 - 2 * step)

    def block(self, offset, core):
        head, z = self.at(offset)
        return (z * CORES + core) * self.heads + head

    def device(self, offset):
        head, z = self.at(offset)
        return {"ctx": z * CORES + self.core, "head": head}


def remote(src, dst, send_sem, recv_sem, device):
    return pltpu.make_async_remote_copy(
        src_ref=src, dst_ref=dst, send_sem=send_sem, recv_sem=recv_sem, device_id=device, device_id_type=MESH
    )


def greet(devices):
    barrier = pltpu.get_barrier_semaphore()
    for device in devices:
        pl.semaphore_signal(barrier, inc=1, device_id=device, device_id_type=MESH)
    pl.semaphore_wait(barrier, len(devices))


def row_chunks(rows):
    if rows % 32 == 0:
        return [pl.ds(0, rows // 2), pl.ds(rows // 2, rows // 2)]
    return [pl.ds(0, rows)]


def line_kernel(chips, key_ref, value_ref, all_keys, all_values, line_send, line_recv, pair_send, pair_recv, own_sem):
    ctx = lax.axis_index("ctx")
    z, core = lax.div(ctx, CORES), lax.rem(ctx, CORES)
    ins, outs = (key_ref, value_ref), (all_keys, all_values)
    partner = {"ctx": z * CORES + 1 - core}
    ways = ((0, 1), (1, -1))

    def inside(spot):
        return (spot >= 0) & (spot < chips)

    barrier = pltpu.get_barrier_semaphore()
    pl.semaphore_signal(barrier, inc=1, device_id=partner, device_id_type=MESH)
    for _, way in ways:

        @pl.when(inside(z + way))
        def _():
            pl.semaphore_signal(
                barrier, inc=1, device_id={"ctx": (z + way) * CORES + core}, device_id_type=MESH
            )

    peers = 1 + sum(jnp.where(inside(z + way), 1, 0) for _, way in ways)
    pl.semaphore_wait(barrier, peers)

    def hop(index, way, step, part):
        block = (z - way * step) * CORES + core
        source = ins[part] if step == 0 else outs[part].at[block]
        return remote(
            source,
            outs[part].at[block],
            line_send.at[index, step, part],
            line_recv.at[index, step, part],
            {"ctx": (z + way) * CORES + core},
        )

    def share(slot, block, part):
        source = ins[part] if slot == 0 else outs[part].at[block]
        return remote(source, outs[part].at[block], pair_send.at[slot, part], pair_recv.at[slot, part], partner)

    def keep(part):
        return pltpu.make_async_copy(ins[part], outs[part].at[ctx], own_sem.at[part])

    for part in (0, 1):
        for index, way in ways:

            @pl.when(inside(z + way))
            def _():
                hop(index, way, 0, part).start()

    for part in (0, 1):
        share(0, ctx, part).start()
        keep(part).start()
    for step in range(1, chips):
        for part in (0, 1):
            for index, way in ways:

                @pl.when(inside(z - way * step))
                def _():
                    hop(index, way, step - 1, part).wait_recv()
                    if step < chips - 1:

                        @pl.when(inside(z + way))
                        def _():
                            hop(index, way, step, part).start()

                    share(index * (chips - 1) + step, (z - way * step) * CORES + core, part).start()

    for part in (0, 1):
        keep(part).wait()
        share(0, ctx, part).wait()
        for index, way in ways:
            for step in range(chips):
                if step < chips - 1:

                    @pl.when(inside(z + way) & inside(z - way * step))
                    def _():
                        hop(index, way, step, part).wait_send()

                if step > 0:

                    @pl.when(inside(z - way * step))
                    def _():
                        share(index * (chips - 1) + step, (z - way * step) * CORES + core, part).wait()


def gather_keys(keys, values):
    n_ctx = lax.axis_size("ctx")
    chips = n_ctx // CORES
    shape = jax.ShapeDtypeStruct((n_ctx,) + keys.shape, keys.dtype)
    slots = 2 * (chips - 1) + 1
    gathered = pl.pallas_call(
        functools.partial(line_kernel, chips),
        out_shape=(shape, shape),
        in_specs=[full_vmem()] * 2,
        out_specs=(full_vmem(),) * 2,
        scratch_shapes=[
            pltpu.SemaphoreType.DMA((2, chips, 2)),
            pltpu.SemaphoreType.DMA((2, chips, 2)),
            pltpu.SemaphoreType.DMA((slots, 2)),
            pltpu.SemaphoreType.DMA((slots, 2)),
            pltpu.SemaphoreType.DMA((2,)),
        ],
        compiler_params=pltpu.CompilerParams(collective_id=0, has_side_effects=True),
        name="gather_keys",
    )(keys, values)
    return [array.reshape(-1, array.shape[-1]) for array in gathered]


def layer_kernel(
    chips, heads, experts, capacity, tile, columns, part_ref, hidden_ref, gain_ref, router_ref, route_ref, up_hbm, down_hbm,
    out_ref, all_ref, residual_ref, hidden_rows, route_rows, lanes_ref, slots, up_ref, down_ref, rows_ref, act_ref,
    gate_ref, back_ref, term_ref, got, outgoing, incoming, weight_sem, head_send, head_recv,
    hop_send, hop_recv, copy_send, copy_recv, pair_send, pair_recv, ring_send, ring_recv,
):
    ring = Ring(chips, heads)
    count, half = ring.count, ring.count // 2
    rows, width = out_ref.shape
    start = width % LANES
    chunks = row_chunks(rows)
    parts = range(len(chunks))
    ways = ((0, 1), (1, -1))
    turned = (((1,), (1,)), ((), ()))
    ctx, head = lax.axis_index("ctx"), ring.head
    others = [{"ctx": ctx, "head": lax.rem(head + turn, heads)} for turn in range(1, heads)]

    greet([ring.device(1), ring.device(-1), ring.partner] + others)
    sends = []
    for turn, device in enumerate(others):
        target = pl.ds(pl.multiple_of(device["head"] * rows, rows), rows)
        copy = remote(part_ref.at[target], slots.at[turn], head_send.at[turn], head_recv.at[turn], device)
        copy.start()
        sends.append(copy)

    loads = [
        pltpu.make_async_copy(up_hbm, up_ref, weight_sem.at[0]),
        pltpu.make_async_copy(down_hbm, down_ref, weight_sem.at[1]),
    ]
    for copy in loads:
        copy.start()

    own = pl.ds(pl.multiple_of(head * rows, rows), rows)
    hidden_rows[...] = hidden_ref[...].T
    tokens = route_ref.shape[1]
    eye = (
        lax.broadcasted_iota(jnp.int32, (tokens, tokens), 0) == lax.broadcasted_iota(jnp.int32, (tokens, tokens), 1)
    ).astype(jnp.float32)
    route_rows[...] = lax.dot_general(
        eye.astype(jnp.bfloat16),
        route_ref[...].astype(jnp.float32).astype(jnp.bfloat16),
        turned,
        preferred_element_type=jnp.float32,
    )
    lanes_ref[...] = jnp.zeros(lanes_ref.shape, lanes_ref.dtype)
    lanes_ref[start : start + experts, :] = router_ref[...]
    lanes_ref[start + experts : start + 2 * experts, :] = router_ref[...]

    total = hidden_rows[own, :].astype(jnp.float32) + part_ref[own, :].astype(jnp.float32)
    for turn, copy in enumerate(sends):
        copy.wait_recv()
        total = total + slots[turn].astype(jnp.float32)
    residual = total.astype(jnp.bfloat16)
    residual_ref[...] = residual
    wide = residual.astype(jnp.float32)
    scale = lax.rsqrt(jnp.mean(wide * wide, axis=-1, keepdims=True) + 1e-05)
    normed = (wide * scale * gain_ref[...]).astype(jnp.bfloat16)

    logits = lax.dot_general(normed, lanes_ref[...], turned, preferred_element_type=jnp.float32)
    lane = lax.broadcasted_iota(jnp.int32, logits.shape, 1) - start
    first = (lane >= 0) & (lane < experts)
    third = (lane >= 2 * experts) & (lane < 3 * experts)
    names = route_rows[own, :]
    present = jnp.zeros(logits.shape, jnp.bool_)
    named = jnp.zeros(logits.shape, jnp.bool_)
    spot = lane.astype(jnp.float32)
    for k in range(route_ref.shape[0]):
        name = names[:, k : k + 1]
        present = present | (spot == name) | (spot - experts == name)
        named = named | (spot - 2 * experts == name)
    top = jnp.max(jnp.where(present, logits, -jnp.inf), axis=-1, keepdims=True)
    powers = jnp.where(present, jnp.exp(jnp.where(present, logits - top, 0.0)), 0.0)
    gates = powers / jnp.sum(jnp.where(first, powers, 0.0), axis=-1, keepdims=True)
    coarse = gates.astype(jnp.bfloat16)
    rest = gates - coarse.astype(jnp.float32)
    earlier = lax.broadcasted_iota(jnp.int32, (rows, rows), 0) > lax.broadcasted_iota(jnp.int32, (rows, rows), 1)
    rank = jnp.dot(
        earlier.astype(jnp.float32).astype(jnp.bfloat16),
        named.astype(jnp.float32).astype(jnp.bfloat16),
        preferred_element_type=jnp.float32,
    )
    rank = jnp.where(named, rank, -1.0)
    tail = jnp.where(third, rank, jnp.where(first, coarse.astype(jnp.float32), rest))
    mine = ring.block(0, ring.core)
    all_ref[mine, :, width - start :] = tail.astype(jnp.bfloat16)
    all_ref[mine, :, :width] = normed

    def last(index, j):
        return (j == 0) == (index == 0)

    def hop(index, way, step, j):
        view = all_ref.at[ring.block(-way * step, ring.core), chunks[j]]
        return remote(view, view, hop_send.at[index, step, j], hop_recv.at[index, step, j], ring.device(way))

    def relay(slot, offset, j):
        view = all_ref.at[ring.block(offset, ring.core), chunks[j]]
        return remote(view, view, copy_send.at[slot, j], copy_recv.at[slot, j], ring.partner)

    def forward(step, j):
        for index, way in ways:
            if isinstance(step, int) and step == half and not last(index, j):
                continue
            hop(index, way, step - 1, j).wait_recv()
            if last(index, j):
                if not (isinstance(step, int) and step == half):
                    hop(index, way, step, j).start()
            elif not isinstance(step, int):

                @pl.when(step < half - 1)
                def _():
                    hop(index, way, step, j).start()

            elif step < half - 1:
                hop(index, way, step, j).start()
            relay(index * half + step, -way * step, j).start()

    def share(slot, offset):
        return remote(
            term_ref.at[ring.block(offset, 1 - ring.core)], got.at[slot], pair_send.at[slot], pair_recv.at[slot], ring.partner
        )

    def compute(offsets, hooks):
        blocks = [ring.block(offset, core) for offset in offsets for core in range(CORES)]
        used = len(blocks) * capacity
        expert = ctx
        for i, block in enumerate(blocks):
            tail = all_ref[block, :, width - start :]
            lane = lax.broadcasted_iota(jnp.int32, (LANES, LANES), 1) - start
            line = lax.broadcasted_iota(jnp.int32, (LANES, LANES), 0)
            pick = ((line == 0) & ((lane == expert) | (lane == expert + experts))) | (
                (line == 1) & (lane == expert + 2 * experts)
            )
            across = lax.dot_general(
                pick.astype(jnp.float32).astype(jnp.bfloat16), tail, turned, preferred_element_type=jnp.float32
            )
            slot = lax.broadcasted_iota(jnp.int32, (capacity, rows), 0).astype(jnp.float32)
            match = across[1:2] == slot
            gate = jnp.sum(jnp.where(match, across[:1], 0.0), axis=1, keepdims=True)
            here = lax.broadcasted_iota(jnp.int32, (rows, LANES), 1) - start == expert + 2 * experts
            down_rank = jnp.sum(jnp.where(here, tail.astype(jnp.float32), 0.0), axis=1, keepdims=True)
            slot_down = lax.broadcasted_iota(jnp.int32, (rows, capacity), 1).astype(jnp.float32)
            span = slice(i * capacity, (i + 1) * capacity)
            picked = jnp.dot(
                match.astype(jnp.float32).astype(jnp.bfloat16), all_ref[block, :, :width], preferred_element_type=jnp.float32
            )
            rows_ref[span, :] = picked.astype(jnp.bfloat16)
            gate_ref[span, :] = gate
            back_ref[i] = (down_rank == slot_down).astype(jnp.float32).astype(jnp.bfloat16)

        def multiply(t, carry):
            span = pl.ds(pl.multiple_of(t * tile, 8), tile)
            x = rows_ref[:used, :]
            a = lax.dot_general(x, up_ref[0, span, :], turned, preferred_element_type=jnp.float32)
            b = lax.dot_general(x, up_ref[1, span, :], turned, preferred_element_type=jnp.float32)
            act_ref[t, :used, :] = (a * jax.nn.sigmoid(1.702 * a) * (b + 1.0)).astype(jnp.bfloat16)
            for spot, hook in enumerate(hooks):

                @pl.when(t == spot)
                def _():
                    hook()

            return carry

        lax.fori_loop(0, act_ref.shape[0], multiply, 0)
        for first in range(0, width, columns):
            span = slice(first, min(first + columns, width))
            piece = 0.0
            for t in range(act_ref.shape[0]):
                piece = piece + jnp.dot(
                    act_ref[t, :used, :], down_ref[t * tile : (t + 1) * tile, span], preferred_element_type=jnp.float32
                )
            gated = (piece * gate_ref[:used, :]).astype(jnp.bfloat16)
            for i, block in enumerate(blocks):
                term = jnp.dot(back_ref[i], gated[i * capacity : (i + 1) * capacity], preferred_element_type=jnp.float32)
                term_ref[block, :, span] = term.astype(jnp.bfloat16)

    for j in parts:
        for index, way in ways:
            if half > 1 or last(index, j):
                hop(index, way, 0, j).start()
        relay(0, 0, j).start()
    for copy in loads:
        copy.wait()
    for j in parts:
        relay(0, 0, j).wait_recv()
    compute([0], [])
    share(0, 0).start()
    for j in parts:
        forward(1, j)

    def ready(distance):
        for index, way in ways:
            for j in parts:
                relay(index * half + distance, -way * distance, j).wait_recv()

    def pair_up(distance):
        for index, way in ways:
            share(index * half + distance, -way * distance).start()

    def travel(distance, carry):
        ready(distance)
        compute(
            [-way * distance for index, way in ways], [functools.partial(forward, distance + 1, j) for j in parts]
        )
        pair_up(distance)
        return carry

    lax.fori_loop(1, half - 1, travel, 0)
    ready(half - 1)
    compute([1 - half, half - 1], [functools.partial(forward, half, j) for j in parts])
    pair_up(half - 1)
    for j in parts:
        for index, way in ways:
            if last(index, j):
                relay(index * half + half, -way * half, j).wait_recv()
    compute([half], [])
    share(half, half).start()

    arrived, hops = set(), {}

    def slot_of(offset):
        return offset + half if 0 < offset < half else abs(offset)

    def pair(offset, chunk):
        offset = half if offset == -half else offset
        if offset not in arrived:
            share(slot_of(offset), offset).wait_recv()
            arrived.add(offset)
        mine = term_ref[ring.block(offset, ring.core), chunk, :].astype(jnp.float32)
        return mine + got[slot_of(offset), chunk, :].astype(jnp.float32)

    for step in range(half):
        for j, chunk in enumerate(chunks):
            for index, way in ways:
                if step == 0 and not last(index, j):
                    continue
                total = pair(way * (half - step), chunk)
                if (index, step - 1, j) in hops:
                    hops[index, step - 1, j].wait_recv()
                    total = total + incoming[index, step - 1, chunk, :].astype(jnp.float32)
                outgoing[index, step, chunk, :] = total.astype(jnp.bfloat16)
                hops[index, step, j] = remote(
                    outgoing.at[index, step, chunk],
                    incoming.at[index, step, chunk],
                    ring_send.at[index, step, j],
                    ring_recv.at[index, step, j],
                    ring.device(way),
                )
                hops[index, step, j].start()
    for j, chunk in enumerate(chunks):
        total = pair(0, chunk) + residual_ref[chunk, :].astype(jnp.float32)
        for index in (0, 1):
            if (index, half - 1, j) in hops:
                hops[index, half - 1, j].wait_recv()
                total = total + incoming[index, half - 1, chunk, :].astype(jnp.float32)
        out_ref[chunk, :] = total.astype(jnp.bfloat16)

    for copy in sends + list(hops.values()):
        copy.wait_send()
    share(0, 0).wait_send()
    share(half, half).wait_send()
    for j in parts:
        relay(0, 0, j).wait_send()
        for index, way in ways:
            if last(index, j):
                hop(index, way, half - 1, j).wait_send()
                relay(index * half + half, -way * half, j).wait_send()
            hop(index, way, 0, j).wait_send()

    def drain(step, carry):
        for index, way in ways:
            share(index * half + step, -way * step).wait_send()
            for j in parts:
                relay(index * half + step, -way * step, j).wait_send()

                @pl.when(step < half - 1)
                def _():
                    hop(index, way, step, j).wait_send()

        return carry

    lax.fori_loop(1, half, drain, 0)


def norm_and_experts(partial_sums, hidden, norm_gain, router, routes, w_gate_up, w_down, capacity):
    chips, heads = lax.axis_size("ctx") // CORES, lax.axis_size("head")
    tokens, width = hidden.shape
    rows = tokens // heads
    experts = router.shape[1]
    hidden_units = w_down.shape[1]
    padded = width - width % LANES + LANES
    half = chips * heads // 2
    blocks = chips * heads * CORES
    parts = len(row_chunks(rows))
    capacity = -(-capacity // 16) * 16
    tile = hidden_units // 3 if hidden_units % 48 == 0 else hidden_units
    columns = 8 * LANES
    most = 2 * CORES
    bf16, f32, dma = jnp.bfloat16, jnp.float32, pltpu.SemaphoreType.DMA
    anywhere = pl.BlockSpec(memory_space=pl.ANY)
    return pl.pallas_call(
        functools.partial(layer_kernel, chips, heads, experts, capacity, tile, columns),
        out_shape=jax.ShapeDtypeStruct((rows, width), bf16),
        in_specs=[full_vmem()] * 5 + [anywhere] * 2,
        out_specs=full_vmem(),
        scratch_shapes=[
            pltpu.VMEM((blocks, rows, padded), bf16),
            pltpu.VMEM((rows, width), bf16),
            pltpu.VMEM((tokens, width), bf16),
            pltpu.VMEM((tokens, routes.shape[1]), f32),
            pltpu.VMEM((LANES, width), bf16),
            pltpu.VMEM((heads - 1, rows, width), bf16),
            pltpu.VMEM((2, hidden_units, width), bf16),
            pltpu.VMEM((hidden_units, width), bf16),
            pltpu.VMEM((most * capacity, width), bf16),
            pltpu.VMEM((hidden_units // tile, most * capacity, tile), bf16),
            pltpu.VMEM((most * capacity, 1), f32),
            pltpu.VMEM((most, rows, capacity), bf16),
            pltpu.VMEM((blocks, rows, width), bf16),
            pltpu.VMEM((2 * half, rows, width), bf16),
            pltpu.VMEM((2, half, rows, width), bf16),
            pltpu.VMEM((2, half, rows, width), bf16),
            dma((2,)),
            dma((heads - 1,)),
            dma((heads - 1,)),
            dma((2, half, parts)),
            dma((2, half, parts)),
            dma((2 * half + 1, parts)),
            dma((2 * half + 1, parts)),
            dma((2 * half,)),
            dma((2 * half,)),
            dma((2, half, parts)),
            dma((2, half, parts)),
        ],
        compiler_params=pltpu.CompilerParams(
            collective_id=1, has_side_effects=True, vmem_limit_bytes=60 * 1024 * 1024
        ),
        name="norm_and_experts",
    )(
        partial_sums,
        hidden.T,
        norm_gain.reshape(1, -1),
        router.T,
        routes.T,
        jnp.swapaxes(w_gate_up[0], 1, 2),
        w_down[0],
    )


def body(
    queries,
    keys,
    values,
    sinks,
    segments,
    hidden_in,
    routes,
    w_out,
    norm_gain,
    router,
    w_gate_up,
    w_down,
):
    n_ctx = lax.axis_size("ctx")
    n_head = lax.axis_size("head")
    tok_count = queries.shape[0]
    top_count = routes.shape[1]
    q_start = lax.axis_index("ctx") * tok_count
    tok_pos = q_start + jnp.arange(tok_count, dtype=jnp.int32)
    tok_seg = lax.dynamic_slice_in_dim(segments, q_start, tok_count, 0)
    all_keys, all_values = gather_keys(keys, values)
    attended = attend(queries, all_keys, all_values, sinks, tok_pos, tok_seg, segments)
    capacity = max(2, min(tok_count // n_head, 3 * tok_count * top_count // (2 * n_head * n_ctx)))
    partial_sums = jnp.dot(attended, w_out, preferred_element_type=jnp.float32).astype(jnp.bfloat16)
    return norm_and_experts(partial_sums, hidden_in, norm_gain, router, routes, w_gate_up, w_down, capacity)


def solution(mesh):
    placed = (
        P(("group", "ctx"), "head"),
        P(("group", "ctx"), "head"),
        P(("group", "ctx"), "head"),
        P("head"),
        P("group"),
        P(("group", "ctx"), None),
        P(("group", "ctx"), None),
        P("head", None),
        P(),
        P(),
        P("ctx", None, None, "head"),
        P("ctx", "head", None),
    )
    return jax.shard_map(
        body,
        mesh=mesh,
        in_specs=placed,
        out_specs=P(("group", "ctx", "head"), None),
        check_vma=False,
    )
```

profile of v0, /device:TPU:0, one launch (start us, length us, event | category | flops | bytes accessed | tf_op | source)
XLA Modules:
  0.0 149.3 jit_solution(1224103864883480460)
XLA Ops:
  0.0 0.0 copy-start
  0.0 0.8 dynamic-slice_bitcast_fusion
  0.8 0.7 copy.15.own_segment_ref
  1.5 0.6 iota_add_fusion.place_ref
  2.1 18.6 %gather_keys.1 = (bf16[8,128,256]{2,1,0:T(8,128)(2,1)}, bf16[8,128,256]{2,1,0:T(8,128)(2,1)}) custom-call(bf16[128,256]{1,0:T(8,128)(2,1)} %key_ref.1, bf16[128,256]{1,0:T(8,128)(2,1)} %value_ref.1), custom_call_target="tpu_custom_call" | custom-call | tf_op jit(solution)/shard_map/gather_keys/pallas_call | solution.py:208
  20.8 18.3 %attend.1 = bf16[128,2048]{1,0:T(8,128)(2,1)} custom-call(bf16[128,2048]{1,0:T(8,128)(2,1)} %query_ref.1, bf16[1024,256]{1,0:T(8,128)(2,1)} %bitcast.18, bf16[1024,256]{1,0:T(8,128)(2,1)} %bitcast.19, f32[1,32]{1,0:T(1,128)} %bitcast.23, s32[128,1]{1,0:T(8,128)} %iota_add_fusion.place_ref, s32[1,1024]{1,0:T(1,128)} %bitcast.21, s32[128,1]{1,0:T(8,128)} %copy.15.own_segment_ref), custom_call_target="tpu_custom_call" | custom-call | tf_op jit(solution)/shard_map/attend/pallas_call | solution.py:49
  39.1 8.0 %convolution_convert_fusion = bf16[128,2880]{0,1:T(8,128)(2,1)S(1)} fusion(bf16[128,2048]{1,0:T(8,128)(2,1)} %attend.1, bf16[2048,2880]{0,1:T(8,128)(2,1)} %param.19), kind=kOutput, calls=%fused_computation | convolution fusion | flops 1510318080 | bytes 13058048 | tf_op jit(solution)/shard_map/dot_general | solution.py:599
  47.0 1.1 copy.16.part_ref
  48.2 0.0 copy-done
  48.2 0.6 reshape.31.gain_ref
  48.8 98.8 %norm_and_experts.1 = bf16[64,2880]{1,0:T(8,128)(2,1)} custom-call(bf16[128,2880]{1,0:T(8,128)(2,1)} %copy.16.part_ref, bf16[2880,128]{1,0:T(8,128)(2,1)} %bitcast.17, f32[1,2880]{1,0:T(1,128)} %reshape.31.gain_ref, bf16[8,2880]{1,0:T(8,128)(2,1)} %bitcast.20, s32[4,128]{1,0:T(4,128)} %bitcast.22, bf16[2,1440,2880]{2,1,0:T(8,128)(2,1)} %bitcast.15, ...), custom_call_target="tpu_custom_call" | custom-call | tf_op jit(solution)/shard_map/norm_and_experts/pallas_call | solution.py:526
  147.6 1.8 %copy.18 = bf16[64,2880]{1,0:T(8,128)(2,1)} copy(bf16[64,2880]{1,0:T(8,128)(2,1)} %norm_and_experts.1) | data formatting | bytes 737280
Async XLA Ops:
  0.0 48.2 %copy-start = (f32[2880]{0:T(1024)S(1)}, f32[2880]{0:T(1024)}, u32[]{:S(2)}) copy-start(f32[2880]{0:T(1024)} %param.20) | copy-start | bytes 34564
where the time goes:
time: 150 us; the launch traced here: 149 us
  Pallas kernels  136 us (91%)
  matrix products  7.95 us (5%)
  local copies, waits for them, and re-layouts  5.02 us (3%)
    pallas_call x1, Pallas kernels, norm_and_experts(): pl.pallas_call(functools.partial(layer_kernel, chips, heads, experts, cap...  98.8 us
    pallas_call x1, Pallas kernels, gather_keys(): pl.pallas_call(functools.partial(line_kernel, chips), out_shape=(shape, s...  18.6 us
    pallas_call x1, Pallas kernels, attend(): pl.pallas_call(attend_kernel, out_shape=jax.ShapeDtypeStruct(queries.shap...  18.3 us
    dot_general x1, matrix products, body(): jnp.dot(attended, w_out, preferred_element_type=jnp.float32)  7.95 us

commit v1 on v0

--- a/solution.py
+++ b/solution.py
@@ -1,4 +1,5 @@
 import functools
+import math
 
 import jax
 import jax.numpy as jnp
@@ -11,56 +12,6 @@
 
 
 masked_value = -1e30
-
-
-def attend_kernel(
-    query_ref, key_ref, value_ref, sink_ref, place_ref, segment_ref, own_segment_ref, out_ref
-):
-    rows = query_ref.shape[0]
-    kv_groups = key_ref.shape[1] // HEAD_SIZE
-    share = query_ref.shape[1] // key_ref.shape[1]
-    spot = lax.broadcasted_iota(jnp.int32, (rows, key_ref.shape[0]), 1)
-    visible = (spot <= place_ref[...]) & (segment_ref[...] == own_segment_ref[...])
-    hidden_bias = jnp.where(visible, 0.0, masked_value)
-    for group in range(kv_groups):
-        span = slice(group * HEAD_SIZE, (group + 1) * HEAD_SIZE)
-        group_keys = key_ref[:, span]
-        group_values = value_ref[:, span]
-        for pair in range(share // 2):
-            both = []
-            for member in range(2):
-                head = group * share + pair * 2 + member
-                query = query_ref[:, head * HEAD_SIZE : (head + 1) * HEAD_SIZE]
-                scores = lax.dot_general(
-                    query, group_keys, (((1,), (1,)), ((), ())), preferred_element_type=jnp.float32
-                )
-                scores = scores * HEAD_SIZE ** (-0.5) + hidden_bias
-                sink = sink_ref[:, head : head + 1]
-                top = jnp.maximum(jnp.max(scores, axis=-1, keepdims=True), sink)
-                weights = jnp.exp(scores - top)
-                total = jnp.sum(weights, axis=-1, keepdims=True) + jnp.exp(sink - top)
-                mixed = jnp.dot(weights.astype(jnp.bfloat16), group_values, preferred_element_type=jnp.float32)
-                both.append((mixed / total).astype(jnp.bfloat16))
-            first = (group * share + pair * 2) * HEAD_SIZE
-            out_ref[:, first : first + 2 * HEAD_SIZE] = jnp.concatenate(both, axis=1)
-
-
-def attend(queries, all_keys, all_values, sinks, tok_pos, tok_seg, segments):
-    return pl.pallas_call(
-        attend_kernel,
-        out_shape=jax.ShapeDtypeStruct(queries.shape, jnp.bfloat16),
-        in_specs=[full_vmem()] * 7,
-        out_specs=full_vmem(),
-        name="attend",
-    )(
-        queries,
-        all_keys,
-        all_values,
-        sinks.reshape(1, -1),
-        tok_pos.reshape(-1, 1),
-        segments.reshape(1, -1),
-        tok_seg.reshape(-1, 1),
-    )
 
 
 MESH = pl.DeviceIdType.MESH
@@ -103,130 +54,282 @@
     )
 
 
-def greet(devices):
-    barrier = pltpu.get_barrier_semaphore()
-    for device in devices:
-        pl.semaphore_signal(barrier, inc=1, device_id=device, device_id_type=MESH)
-    pl.semaphore_wait(barrier, len(devices))
-
-
 def row_chunks(rows):
     if rows % 32 == 0:
         return [pl.ds(0, rows // 2), pl.ds(rows // 2, rows // 2)]
     return [pl.ds(0, rows)]
 
 
-def line_kernel(chips, key_ref, value_ref, all_keys, all_values, line_send, line_recv, pair_send, pair_recv, own_sem):
-    ctx = lax.axis_index("ctx")
+def attend_kernel(
+    chips, heads, key_ref, value_ref, query_ref, sink_ref, segment_ref, hidden_ref, weight_hbm, out_ref,
+    all_keys, all_values, stacked, group_keys, group_values, bias_ref, score_ref, peak_ref, attended_ref, weight_ref,
+    hidden_rows, part_ref, slots,
+    line_send, line_recv, pair_send, pair_recv, head_send, head_recv, weight_sem,
+):
+    ctx, head = lax.axis_index("ctx"), lax.axis_index("head")
     z, core = lax.div(ctx, CORES), lax.rem(ctx, CORES)
-    ins, outs = (key_ref, value_ref), (all_keys, all_values)
+    rows = query_ref.shape[0]
+    groups = key_ref.shape[1] // HEAD_SIZE
+    share = query_ref.shape[1] // key_ref.shape[1]
+    keys = CORES * rows
+    own_rows, width = out_ref.shape
+    ins, alls = (key_ref, value_ref), (all_keys, all_values)
+    turned = (((1,), (1,)), ((), ()))
     partner = {"ctx": z * CORES + 1 - core}
-    ways = ((0, 1), (1, -1))
-
-    def inside(spot):
-        return (spot >= 0) & (spot < chips)
+    above = {"ctx": (z + 1) * CORES + core}
+    others = [{"ctx": ctx, "head": lax.rem(head + turn, heads)} for turn in range(1, heads)]
+    has_above, has_below = z + 1 < chips, z > 0
+    load = pltpu.make_async_copy(weight_hbm, weight_ref, weight_sem)
+    load.start()
 
     barrier = pltpu.get_barrier_semaphore()
-    pl.semaphore_signal(barrier, inc=1, device_id=partner, device_id_type=MESH)
-    for _, way in ways:
-
-        @pl.when(inside(z + way))
+    for device in [partner] + others:
+        pl.semaphore_signal(barrier, inc=1, device_id=device, device_id_type=MESH)
+
+    @pl.when(has_above)
+    def _():
+        pl.semaphore_signal(barrier, inc=1, device_id=above, device_id_type=MESH)
+
+    @pl.when(has_below)
+    def _():
+        pl.semaphore_signal(barrier, inc=1, device_id={"ctx": (z - 1) * CORES + core}, device_id_type=MESH)
+
+    peers = heads + jnp.where(has_above, 1, 0) + jnp.where(has_below, 1, 0)
+    pl.semaphore_wait(barrier, peers)
+
+    def hop(step, part):
+        block = (z - step) * CORES + core
+        source = ins[part] if step == 0 else alls[part].at[block]
+        return remote(source, alls[part].at[block], line_send.at[step, part], line_recv.at[step, part], above)
+
+    def relay(step, part):
+        block = (z - step) * CORES + core
+        source = ins[part] if step == 0 else alls[part].at[block]
+        return remote(source, alls[part].at[block], pair_send.at[step, part], pair_recv.at[step, part], partner)
+
+    for part in (0, 1):
+
+        @pl.when(has_above)
         def _():
-            pl.semaphore_signal(
-                barrier, inc=1, device_id={"ctx": (z + way) * CORES + core}, device_id_type=MESH
+            hop(0, part).start()
+
+        relay(0, part).start()
+    for part in (0, 1):
+        alls[part][ctx] = ins[part][...]
+
+    for index in range(groups * share):
+        span = slice(index * HEAD_SIZE, (index + 1) * HEAD_SIZE)
+        stacked[index // share, index % share * rows : (index % share + 1) * rows, :] = query_ref[:, span]
+    lane = lax.broadcasted_iota(jnp.int32, group_values.shape[1:], 1)
+    for group in range(groups):
+        group_values[group] = (lane == HEAD_SIZE).astype(jnp.float32).astype(jnp.bfloat16)
+    here = pl.ds(pl.multiple_of(ctx * rows, rows), rows)
+    diagonal = lax.broadcasted_iota(jnp.int32, (rows, rows), 0) == lax.broadcasted_iota(jnp.int32, (rows, rows), 1)
+    own_segment = jnp.sum(
+        jnp.where(diagonal, segment_ref[:, here].astype(jnp.float32), 0.0), axis=1, keepdims=True
+    )
+    log2e = math.log2(math.e)
+    factor = HEAD_SIZE ** (-0.5) * log2e
+
+    def score(step):
+        chip = z - step
+        block = all_keys[pl.ds(chip * CORES, CORES)].reshape(keys, key_ref.shape[1])
+        for group in range(groups):
+            group_keys[group] = block[:, group * HEAD_SIZE : (group + 1) * HEAD_SIZE]
+        spot = lax.broadcasted_iota(jnp.int32, (rows, keys), 1) + chip * keys
+        place = lax.broadcasted_iota(jnp.int32, (rows, keys), 0) + ctx * rows
+        segment = segment_ref[:, pl.ds(pl.multiple_of(chip * keys, keys), keys)].astype(jnp.float32)
+        bias_ref[...] = jnp.where((spot <= place) & (segment == own_segment), 0.0, masked_value)
+
+        def one(group, carry):
+            scores = lax.dot_general(stacked[group], group_keys[group], turned, preferred_element_type=jnp.float32)
+            scores = scores.reshape(share, rows, keys) * factor + bias_ref[...]
+            span = pl.ds(group * share, share)
+            score_ref[step, span] = scores
+            peak = scores[:, :, :LANES]
+            for first in range(LANES, keys, LANES):
+                peak = jnp.maximum(peak, scores[:, :, first : first + LANES])
+            peak_ref[span] = peak if step == 0 else jnp.maximum(peak_ref[span], peak)
+            return carry
+
+        lax.fori_loop(0, groups, one, 0)
+
+    def take_values(step):
+        relay(step, 1).wait_recv()
+        block = all_values[pl.ds((z - step) * CORES, CORES)].reshape(keys, value_ref.shape[1])
+        for group in range(groups):
+            group_values[group, step * keys : (step + 1) * keys, :HEAD_SIZE] = block[
+                :, group * HEAD_SIZE : (group + 1) * HEAD_SIZE
+            ]
+
+    relay(0, 0).wait_recv()
+    score(0)
+    for step in range(1, chips):
+
+        @pl.when(z - step >= 0)
+        def _():
+            for part in (0, 1):
+                hop(step - 1, part).wait_recv()
+                if step < chips - 1:
+
+                    @pl.when(has_above)
+                    def _():
+                        hop(step, part).start()
+
+                relay(step, part).start()
+            take_values(step - 1)
+            relay(step, 0).wait_recv()
+            score(step)
+
+        @pl.when(z - step < 0)
+        def _():
+            @pl.when(z - step == -1)
+            def _():
+                take_values(step - 1)
+
+            def blank(index, carry):
+                score_ref[step, index] = jnp.full((rows, keys), masked_value, jnp.float32)
+                return carry
+
+            lax.fori_loop(0, groups * share, blank, 0)
+
+    @pl.when(z == chips - 1)
+    def _():
+        take_values(chips - 1)
+
+    own = pl.ds(pl.multiple_of(head * own_rows, own_rows), own_rows)
+    hidden_rows[...] = hidden_ref[...].T
+
+    def mix(couple, carry):
+        group = lax.div(couple * 2, share)
+        sinks, tops = [], []
+        for member in range(2):
+            sinks.append(sink_ref[couple * 2 + member] * log2e)
+            peak = jnp.max(peak_ref[couple * 2 + member], axis=-1, keepdims=True)
+            tops.append(jnp.maximum(peak, sinks[member]))
+        mixed = jnp.zeros((2 * rows, LANES), jnp.float32)
+        for step in range(chips):
+            weights = jnp.concatenate(
+                [
+                    jnp.exp2(score_ref[step, couple * 2 + member] - tops[member]).astype(jnp.bfloat16)
+                    for member in range(2)
+                ],
+                axis=0,
             )
-
-    peers = 1 + sum(jnp.where(inside(z + way), 1, 0) for _, way in ways)
-    pl.semaphore_wait(barrier, peers)
-
-    def hop(index, way, step, part):
-        block = (z - way * step) * CORES + core
-        source = ins[part] if step == 0 else outs[part].at[block]
-        return remote(
-            source,
-            outs[part].at[block],
-            line_send.at[index, step, part],
-            line_recv.at[index, step, part],
-            {"ctx": (z + way) * CORES + core},
+            mixed = mixed + jnp.dot(
+                weights, group_values[group, step * keys : (step + 1) * keys, :], preferred_element_type=jnp.float32
+            )
+        both = []
+        for member in range(2):
+            mine = mixed[member * rows : (member + 1) * rows]
+            total = mine[:, HEAD_SIZE : HEAD_SIZE + 1] + jnp.exp2(sinks[member] - tops[member])
+            both.append((mine[:, :HEAD_SIZE] / total).astype(jnp.bfloat16))
+        span = pl.ds(pl.multiple_of(couple * 2 * HEAD_SIZE, 2 * HEAD_SIZE), 2 * HEAD_SIZE)
+        attended_ref[:, span] = jnp.concatenate(both, axis=1)
+        return carry
+
+    lax.fori_loop(0, groups * share // 2, mix, 0)
+
+    load.wait()
+    spans = column_spans(part_ref.shape[1])
+    part_ref[:, spans[-1][0] :] = jnp.zeros((rows, spans[-1][1]), part_ref.dtype)
+    sends = {}
+    for c, (first, size) in enumerate(spans):
+        last = min(first + size, width)
+        piece = lax.dot_general(
+            attended_ref[...], weight_ref[first:last, :], turned, preferred_element_type=jnp.float32
         )
-
-    def share(slot, block, part):
-        source = ins[part] if slot == 0 else outs[part].at[block]
-        return remote(source, outs[part].at[block], pair_send.at[slot, part], pair_recv.at[slot, part], partner)
-
-    def keep(part):
-        return pltpu.make_async_copy(ins[part], outs[part].at[ctx], own_sem.at[part])
-
+        part_ref[:, first:last] = piece.astype(jnp.bfloat16)
+        for turn, device in enumerate(others):
+            target = pl.ds(pl.multiple_of(device["head"] * own_rows, own_rows), own_rows)
+            sends[turn, c] = remote(
+                part_ref.at[target, pl.ds(first, size)],
+                slots.at[turn, :, pl.ds(first, size)],
+                head_send.at[turn, c],
+                head_recv.at[turn, c],
+                device,
+            )
+            sends[turn, c].start()
+    for c, (first, size) in enumerate(spans):
+        span = slice(first, min(first + size, width))
+        total = hidden_rows[own, span].astype(jnp.float32) + part_ref[own, span].astype(jnp.float32)
+        for turn in range(heads - 1):
+            sends[turn, c].wait_recv()
+            total = total + slots[turn, :, span].astype(jnp.float32)
+        out_ref[:, span] = total.astype(jnp.bfloat16)
+
+    for copy in sends.values():
+        copy.wait_send()
     for part in (0, 1):
-        for index, way in ways:
-
-            @pl.when(inside(z + way))
+        for step in range(chips):
+
+            @pl.when(z - step >= 0)
             def _():
-                hop(index, way, 0, part).start()
-
-    for part in (0, 1):
-        share(0, ctx, part).start()
-        keep(part).start()
-    for step in range(1, chips):
-        for part in (0, 1):
-            for index, way in ways:
-
-                @pl.when(inside(z - way * step))
-                def _():
-                    hop(index, way, step - 1, part).wait_recv()
-                    if step < chips - 1:
-
-                        @pl.when(inside(z + way))
-                        def _():
-                            hop(index, way, step, part).start()
-
-                    share(index * (chips - 1) + step, (z - way * step) * CORES + core, part).start()
-
-    for part in (0, 1):
-        keep(part).wait()
-        share(0, ctx, part).wait()
-        for index, way in ways:
-            for step in range(chips):
+                relay(step, part).wait_send()
                 if step < chips - 1:
 
-                    @pl.when(inside(z + way) & inside(z - way * step))
+                    @pl.when(has_above)
                     def _():
-                        hop(index, way, step, part).wait_send()
-
-                if step > 0:
-
-                    @pl.when(inside(z - way * step))
-                    def _():
-                        share(index * (chips - 1) + step, (z - way * step) * CORES + core, part).wait()
-
-
-def gather_keys(keys, values):
+                        hop(step, part).wait_send()
+
+
+def column_spans(padded):
+    wide = 8 * LANES
+    return [(first, min(wide, padded - first)) for first in range(0, padded, wide)]
+
+
+def attend(queries, keys, values, sinks, segments, hidden, w_out):
+    chips, heads = lax.axis_size("ctx") // CORES, lax.axis_size("head")
     n_ctx = lax.axis_size("ctx")
-    chips = n_ctx // CORES
-    shape = jax.ShapeDtypeStruct((n_ctx,) + keys.shape, keys.dtype)
-    slots = 2 * (chips - 1) + 1
-    gathered = pl.pallas_call(
-        functools.partial(line_kernel, chips),
-        out_shape=(shape, shape),
-        in_specs=[full_vmem()] * 2,
-        out_specs=(full_vmem(),) * 2,
+    rows = queries.shape[0]
+    width = w_out.shape[1]
+    padded = -(-width // LANES) * LANES
+    groups = keys.shape[1] // HEAD_SIZE
+    share = queries.shape[1] // keys.shape[1]
+    parts = len(column_spans(padded))
+    bf16, f32, dma = jnp.bfloat16, jnp.float32, pltpu.SemaphoreType.DMA
+    chip_keys = CORES * rows
+    return pl.pallas_call(
+        functools.partial(attend_kernel, chips, heads),
+        out_shape=jax.ShapeDtypeStruct((rows // heads, width), bf16),
+        in_specs=[full_vmem()] * 3
+        + [pl.BlockSpec(memory_space=pltpu.SMEM)]
+        + [full_vmem()] * 2
+        + [pl.BlockSpec(memory_space=pl.ANY)],
+        out_specs=full_vmem(),
         scratch_shapes=[
-            pltpu.SemaphoreType.DMA((2, chips, 2)),
-            pltpu.SemaphoreType.DMA((2, chips, 2)),
-            pltpu.SemaphoreType.DMA((slots, 2)),
-            pltpu.SemaphoreType.DMA((slots, 2)),
-            pltpu.SemaphoreType.DMA((2,)),
+            pltpu.VMEM((n_ctx,) + keys.shape, bf16),
+            pltpu.VMEM((n_ctx,) + keys.shape, bf16),
+            pltpu.VMEM((groups, share * rows, HEAD_SIZE), bf16),
+            pltpu.VMEM((groups, chip_keys, HEAD_SIZE), bf16),
+            pltpu.VMEM((groups, chips * chip_keys, LANES), bf16),
+            pltpu.VMEM((rows, chip_keys), f32),
+            pltpu.VMEM((chips, groups * share, rows, chip_keys), f32),
+            pltpu.VMEM((groups * share, rows, LANES), f32),
+            pltpu.VMEM(queries.shape, bf16),
+            pltpu.VMEM((width, w_out.shape[0]), bf16),
+            pltpu.VMEM((rows, width), bf16),
+            pltpu.VMEM((rows, padded), bf16),
+            pltpu.VMEM((heads - 1, rows // heads, padded), bf16),
+            dma((chips, 2)),
+            dma((chips, 2)),
+            dma((chips, 2)),
+            dma((chips, 2)),
+            dma((heads - 1, parts)),
+            dma((heads - 1, parts)),
+            dma(()),
         ],
-        compiler_params=pltpu.CompilerParams(collective_id=0, has_side_effects=True),
-        name="gather_keys",
-    )(keys, values)
-    return [array.reshape(-1, array.shape[-1]) for array in gathered]
+        compiler_params=pltpu.CompilerParams(
+            collective_id=0, has_side_effects=True, vmem_limit_bytes=60 * 1024 * 1024
+        ),
+        name="attend",
+    )(keys, values, queries, sinks, segments.reshape(1, -1), hidden.T, w_out.T)
 
 
 def layer_kernel(
-    chips, heads, experts, capacity, tile, columns, part_ref, hidden_ref, gain_ref, router_ref, route_ref, up_hbm, down_hbm,
-    out_ref, all_ref, residual_ref, hidden_rows, route_rows, lanes_ref, slots, up_ref, down_ref, rows_ref, act_ref,
-    gate_ref, back_ref, term_ref, got, outgoing, incoming, weight_sem, head_send, head_recv,
+    chips, heads, experts, capacity, tile, columns, residual_ref, gain_ref, router_ref, route_ref, up_hbm, down_hbm,
+    out_ref, all_ref, route_rows, lanes_ref, up_ref, down_ref, rows_ref, act_ref,
+    gate_ref, back_ref, term_ref, got, outgoing, incoming, weight_sem,
     hop_send, hop_recv, copy_send, copy_recv, pair_send, pair_recv, ring_send, ring_recv,
 ):
     ring = Ring(chips, heads)
@@ -238,16 +341,11 @@
     ways = ((0, 1), (1, -1))
     turned = (((1,), (1,)), ((), ()))
     ctx, head = lax.axis_index("ctx"), ring.head
-    others = [{"ctx": ctx, "head": lax.rem(head + turn, heads)} for turn in range(1, heads)]
-
-    greet([ring.device(1), ring.device(-1), ring.partner] + others)
-    sends = []
-    for turn, device in enumerate(others):
-        target = pl.ds(pl.multiple_of(device["head"] * rows, rows), rows)
-        copy = remote(part_ref.at[target], slots.at[turn], head_send.at[turn], head_recv.at[turn], device)
-        copy.start()
-        sends.append(copy)
-
+
+    barrier = pltpu.get_barrier_semaphore()
+    peers = [ring.device(1), ring.device(-1), ring.partner]
+    for device in peers:
+        pl.semaphore_signal(barrier, inc=1, device_id=device, device_id_type=MESH)
     loads = [
         pltpu.make_async_copy(up_hbm, up_ref, weight_sem.at[0]),
         pltpu.make_async_copy(down_hbm, down_ref, weight_sem.at[1]),
@@ -256,7 +354,6 @@
         copy.start()
 
     own = pl.ds(pl.multiple_of(head * rows, rows), rows)
-    hidden_rows[...] = hidden_ref[...].T
     tokens = route_ref.shape[1]
     eye = (
         lax.broadcasted_iota(jnp.int32, (tokens, tokens), 0) == lax.broadcasted_iota(jnp.int32, (tokens, tokens), 1)
@@ -271,12 +368,7 @@
     lanes_ref[start : start + experts, :] = router_ref[...]
     lanes_ref[start + experts : start + 2 * experts, :] = router_ref[...]
 
-    total = hidden_rows[own, :].astype(jnp.float32) + part_ref[own, :].astype(jnp.float32)
-    for turn, copy in enumerate(sends):
-        copy.wait_recv()
-        total = total + slots[turn].astype(jnp.float32)
-    residual = total.astype(jnp.bfloat16)
-    residual_ref[...] = residual
+    residual = residual_ref[...]
     wide = residual.astype(jnp.float32)
     scale = lax.rsqrt(jnp.mean(wide * wide, axis=-1, keepdims=True) + 1e-05)
     normed = (wide * scale * gain_ref[...]).astype(jnp.bfloat16)
@@ -399,6 +491,7 @@
                 term = jnp.dot(back_ref[i], gated[i * capacity : (i + 1) * capacity], preferred_element_type=jnp.float32)
                 term_ref[block, :, span] = term.astype(jnp.bfloat16)
 
+    pl.semaphore_wait(barrier, len(peers))
     for j in parts:
         for index, way in ways:
             if half > 1 or last(index, j):
@@ -480,7 +573,7 @@
                 total = total + incoming[index, half - 1, chunk, :].astype(jnp.float32)
         out_ref[chunk, :] = total.astype(jnp.bfloat16)
 
-    for copy in sends + list(hops.values()):
+    for copy in hops.values():
         copy.wait_send()
     share(0, 0).wait_send()
     share(half, half).wait_send()
@@ -507,10 +600,10 @@
     lax.fori_loop(1, half, drain, 0)
 
 
-def norm_and_experts(partial_sums, hidden, norm_gain, router, routes, w_gate_up, w_down, capacity):
+def norm_and_experts(residual, norm_gain, router, routes, w_gate_up, w_down, capacity):
     chips, heads = lax.axis_size("ctx") // CORES, lax.axis_size("head")
-    tokens, width = hidden.shape
-    rows = tokens // heads
+    rows, width = residual.shape
+    tokens = rows * heads
     experts = router.shape[1]
     hidden_units = w_down.shape[1]
     padded = width - width % LANES + LANES
@@ -526,15 +619,12 @@
     return pl.pallas_call(
         functools.partial(layer_kernel, chips, heads, experts, capacity, tile, columns),
         out_shape=jax.ShapeDtypeStruct((rows, width), bf16),
-        in_specs=[full_vmem()] * 5 + [anywhere] * 2,
+        in_specs=[full_vmem()] * 4 + [anywhere] * 2,
         out_specs=full_vmem(),
         scratch_shapes=[
             pltpu.VMEM((blocks, rows, padded), bf16),
-            pltpu.VMEM((rows, width), bf16),
-            pltpu.VMEM((tokens, width), bf16),
             pltpu.VMEM((tokens, routes.shape[1]), f32),
             pltpu.VMEM((LANES, width), bf16),
-            pltpu.VMEM((heads - 1, rows, width), bf16),
             pltpu.VMEM((2, hidden_units, width), bf16),
             pltpu.VMEM((hidden_units, width), bf16),
             pltpu.VMEM((most * capacity, width), bf16),
@@ -546,8 +636,6 @@
             pltpu.VMEM((2, half, rows, width), bf16),
             pltpu.VMEM((2, half, rows, width), bf16),
             dma((2,)),
-            dma((heads - 1,)),
-            dma((heads - 1,)),
             dma((2, half, parts)),
             dma((2, half, parts)),
             dma((2 * half + 1, parts)),
@@ -562,8 +650,7 @@
         ),
         name="norm_and_experts",
     )(
-        partial_sums,
-        hidden.T,
+        residual,
         norm_gain.reshape(1, -1),
         router.T,
         routes.T,
@@ -590,14 +677,9 @@
     n_head = lax.axis_size("head")
     tok_count = queries.shape[0]
     top_count = routes.shape[1]
-    q_start = lax.axis_index("ctx") * tok_count
-    tok_pos = q_start + jnp.arange(tok_count, dtype=jnp.int32)
-    tok_seg = lax.dynamic_slice_in_dim(segments, q_start, tok_count, 0)
-    all_keys, all_values = gather_keys(keys, values)
-    attended = attend(queries, all_keys, all_values, sinks, tok_pos, tok_seg, segments)
     capacity = max(2, min(tok_count // n_head, 3 * tok_count * top_count // (2 * n_head * n_ctx)))
-    partial_sums = jnp.dot(attended, w_out, preferred_element_type=jnp.float32).astype(jnp.bfloat16)
-    return norm_and_experts(partial_sums, hidden_in, norm_gain, router, routes, w_gate_up, w_down, capacity)
+    residual = attend(queries, keys, values, sinks, segments, hidden_in, w_out)
+    return norm_and_experts(residual, norm_gain, router, routes, w_gate_up, w_down, capacity)
 
 
 def solution(mesh):

time: 150 us -> 134 us (0.89)
  matrix products: 7.95 us -> 0 us
  Pallas kernels: 136 us -> 130 us
  local copies, waits for them, and re-layouts: 5.02 us -> 3.07 us
    dot_general x1 -> x0, matrix products: 7.95 us -> none  [body(): jnp.dot(attended, w_out, preferred_element_type=jnp.float32)]
    pallas_call x2 -> x1, Pallas kernels: 36.9 us -> 29.8 us  [attend(): pl.pallas_call(functools.partial(attend_kernel, chips, heads), out_shape=...]
    pallas_call x1, Pallas kernels: 98.8 us -> 101 us  [norm_and_experts(): pl.pallas_call(functools.partial(layer_kernel, chips, heads, experts, cap...]
where the time goes in v1:
time: 134 us
  Pallas kernels  130 us (97%)
  local copies, waits for them, and re-layouts  3.07 us (2%)
    pallas_call x1, Pallas kernels, norm_and_experts(): pl.pallas_call(functools.partial(layer_kernel, chips, heads, experts, cap...  101 us
    pallas_call x1, Pallas kernels, attend(): pl.pallas_call(functools.partial(attend_kernel, chips, heads), out_shape=...  29.8 us

profile of v1, /device:TPU:0, one launch (start us, length us, event | category | flops | bytes accessed | tf_op | source)
XLA Modules:
  0.0 133.5 jit_solution(2530819894165177376)
XLA Ops:
  0.0 1.3 reshape.7.gain_ref
  1.3 29.8 %attend.1.residual_ref = bf16[64,2880]{1,0:T(8,128)(2,1)} custom-call(bf16[128,256]{1,0:T(8,128)(2,1)} %key_ref.1, bf16[128,256]{1,0:T(8,128)(2,1)} %value_ref.1, bf16[128,2048]{1,0:T(8,128)(2,1)} %query_ref.1, f32[32]{0:T(128)} %sink_ref.1, s32[1,1024]{1,0:T(1,128)} %bitcast.14, bf16[2880,128]{1,0:T(8,128)(2,1)} %bitcast.12, bf16[2880,2048]{1,0:T(8,128)(2,1)} %bitcast.10), custom_call_target="tpu_custom_call" | custom-call | tf_op jit(solution)/shard_map/attend/pallas_call | solution.py:292
  31.1 100.7 %norm_and_experts.1 = bf16[64,2880]{1,0:T(8,128)(2,1)} custom-call(bf16[64,2880]{1,0:T(8,128)(2,1)} %attend.1.residual_ref, f32[1,2880]{1,0:T(1,128)} %reshape.7.gain_ref, bf16[8,2880]{1,0:T(8,128)(2,1)} %bitcast.13, s32[4,128]{1,0:T(4,128)} %bitcast.15, bf16[2,1440,2880]{2,1,0:T(8,128)(2,1)} %bitcast.9, bf16[1440,2880]{1,0:T(8,128)(2,1)} %bitcast.11), custom_call_target="tpu_custom_call" | custom-call | tf_op jit(solution)/shard_map/norm_and_experts/pallas_call | solution.py:619
  131.8 1.8 %copy.14 = bf16[64,2880]{1,0:T(8,128)(2,1)} copy(bf16[64,2880]{1,0:T(8,128)(2,1)} %norm_and_experts.1) | data formatting | bytes 737280

commit v2 on v1

--- a/solution.py
+++ b/solution.py
@@ -327,9 +327,8 @@
 
 
 def layer_kernel(
-    chips, heads, experts, capacity, tile, columns, residual_ref, gain_ref, router_ref, route_ref, up_hbm, down_hbm,
-    out_ref, all_ref, route_rows, lanes_ref, up_ref, down_ref, rows_ref, act_ref,
-    gate_ref, back_ref, term_ref, got, outgoing, incoming, weight_sem,
+    chips, heads, experts, tile, columns, residual_ref, gain_ref, router_ref, route_ref, up_hbm, down_hbm,
+    out_ref, all_ref, route_rows, lanes_ref, up_ref, down_ref, act_ref, term_ref, got, outgoing, incoming, weight_sem,
     hop_send, hop_recv, copy_send, copy_recv, pair_send, pair_recv, ring_send, ring_recv,
 ):
     ring = Ring(chips, heads)
@@ -346,12 +345,20 @@
     peers = [ring.device(1), ring.device(-1), ring.partner]
     for device in peers:
         pl.semaphore_signal(barrier, inc=1, device_id=device, device_id_type=MESH)
-    loads = [
-        pltpu.make_async_copy(up_hbm, up_ref, weight_sem.at[0]),
-        pltpu.make_async_copy(down_hbm, down_ref, weight_sem.at[1]),
-    ]
-    for copy in loads:
-        copy.start()
+    tiles = act_ref.shape[0]
+
+    def load_up(t):
+        span = pl.ds(pl.multiple_of(t * tile, 8), tile)
+        return [
+            pltpu.make_async_copy(up_hbm.at[which, span], up_ref.at[which, span], weight_sem.at[which, t])
+            for which in range(2)
+        ]
+
+    load_down = pltpu.make_async_copy(down_hbm, down_ref, weight_sem.at[2, 0])
+    for t in range(tiles):
+        for copy in load_up(t):
+            copy.start()
+    load_down.start()
 
     own = pl.ds(pl.multiple_of(head * rows, rows), rows)
     tokens = route_ref.shape[1]
@@ -371,33 +378,23 @@
     residual = residual_ref[...]
     wide = residual.astype(jnp.float32)
     scale = lax.rsqrt(jnp.mean(wide * wide, axis=-1, keepdims=True) + 1e-05)
-    normed = (wide * scale * gain_ref[...]).astype(jnp.bfloat16)
+    normed = (wide * scale * gain_ref[...][None, :]).astype(jnp.bfloat16)
 
     logits = lax.dot_general(normed, lanes_ref[...], turned, preferred_element_type=jnp.float32)
     lane = lax.broadcasted_iota(jnp.int32, logits.shape, 1) - start
     first = (lane >= 0) & (lane < experts)
-    third = (lane >= 2 * experts) & (lane < 3 * experts)
     names = route_rows[own, :]
     present = jnp.zeros(logits.shape, jnp.bool_)
-    named = jnp.zeros(logits.shape, jnp.bool_)
     spot = lane.astype(jnp.float32)
     for k in range(route_ref.shape[0]):
         name = names[:, k : k + 1]
         present = present | (spot == name) | (spot - experts == name)
-        named = named | (spot - 2 * experts == name)
     top = jnp.max(jnp.where(present, logits, -jnp.inf), axis=-1, keepdims=True)
     powers = jnp.where(present, jnp.exp(jnp.where(present, logits - top, 0.0)), 0.0)
     gates = powers / jnp.sum(jnp.where(first, powers, 0.0), axis=-1, keepdims=True)
     coarse = gates.astype(jnp.bfloat16)
     rest = gates - coarse.astype(jnp.float32)
-    earlier = lax.broadcasted_iota(jnp.int32, (rows, rows), 0) > lax.broadcasted_iota(jnp.int32, (rows, rows), 1)
-    rank = jnp.dot(
-        earlier.astype(jnp.float32).astype(jnp.bfloat16),
-        named.astype(jnp.float32).astype(jnp.bfloat16),
-        preferred_element_type=jnp.float32,
-    )
-    rank = jnp.where(named, rank, -1.0)
-    tail = jnp.where(third, rank, jnp.where(first, coarse.astype(jnp.float32), rest))
+    tail = jnp.where(first, coarse.astype(jnp.float32), rest)
     mine = ring.block(0, ring.core)
     all_ref[mine, :, width - start :] = tail.astype(jnp.bfloat16)
     all_ref[mine, :, :width] = normed
@@ -436,60 +433,47 @@
             term_ref.at[ring.block(offset, 1 - ring.core)], got.at[slot], pair_send.at[slot], pair_recv.at[slot], ring.partner
         )
 
-    def compute(offsets, hooks):
+    def compute(offsets, hooks, fresh=False):
         blocks = [ring.block(offset, core) for offset in offsets for core in range(CORES)]
-        used = len(blocks) * capacity
-        expert = ctx
-        for i, block in enumerate(blocks):
-            tail = all_ref[block, :, width - start :]
-            lane = lax.broadcasted_iota(jnp.int32, (LANES, LANES), 1) - start
-            line = lax.broadcasted_iota(jnp.int32, (LANES, LANES), 0)
-            pick = ((line == 0) & ((lane == expert) | (lane == expert + experts))) | (
-                (line == 1) & (lane == expert + 2 * experts)
-            )
-            across = lax.dot_general(
-                pick.astype(jnp.float32).astype(jnp.bfloat16), tail, turned, preferred_element_type=jnp.float32
-            )
-            slot = lax.broadcasted_iota(jnp.int32, (capacity, rows), 0).astype(jnp.float32)
-            match = across[1:2] == slot
-            gate = jnp.sum(jnp.where(match, across[:1], 0.0), axis=1, keepdims=True)
-            here = lax.broadcasted_iota(jnp.int32, (rows, LANES), 1) - start == expert + 2 * experts
-            down_rank = jnp.sum(jnp.where(here, tail.astype(jnp.float32), 0.0), axis=1, keepdims=True)
-            slot_down = lax.broadcasted_iota(jnp.int32, (rows, capacity), 1).astype(jnp.float32)
-            span = slice(i * capacity, (i + 1) * capacity)
-            picked = jnp.dot(
-                match.astype(jnp.float32).astype(jnp.bfloat16), all_ref[block, :, :width], preferred_element_type=jnp.float32
-            )
-            rows_ref[span, :] = picked.astype(jnp.bfloat16)
-            gate_ref[span, :] = gate
-            back_ref[i] = (down_rank == slot_down).astype(jnp.float32).astype(jnp.bfloat16)
+        used = len(blocks) * rows
+        gates = []
+        for block in blocks:
+            tail = all_ref[block, :, width - start :].astype(jnp.float32)
+            lane = lax.broadcasted_iota(jnp.int32, tail.shape, 1) - start
+            here = (lane == ctx) | (lane == ctx + experts)
+            gates.append(jnp.sum(jnp.where(here, tail, 0.0), axis=1, keepdims=True))
+        gate = jnp.concatenate(gates, axis=0)
 
         def multiply(t, carry):
+            if fresh:
+                for copy in load_up(t):
+                    copy.wait()
             span = pl.ds(pl.multiple_of(t * tile, 8), tile)
-            x = rows_ref[:used, :]
+            x = jnp.concatenate([all_ref[block, :, :width] for block in blocks], axis=0)
             a = lax.dot_general(x, up_ref[0, span, :], turned, preferred_element_type=jnp.float32)
             b = lax.dot_general(x, up_ref[1, span, :], turned, preferred_element_type=jnp.float32)
             act_ref[t, :used, :] = (a * jax.nn.sigmoid(1.702 * a) * (b + 1.0)).astype(jnp.bfloat16)
             for spot, hook in enumerate(hooks):
 
-                @pl.when(t == spot)
+                @pl.when(t == min(spot, tiles - 1))
                 def _():
                     hook()
 
             return carry
 
-        lax.fori_loop(0, act_ref.shape[0], multiply, 0)
+        lax.fori_loop(0, tiles, multiply, 0)
+        if fresh:
+            load_down.wait()
         for first in range(0, width, columns):
             span = slice(first, min(first + columns, width))
             piece = 0.0
-            for t in range(act_ref.shape[0]):
+            for t in range(tiles):
                 piece = piece + jnp.dot(
                     act_ref[t, :used, :], down_ref[t * tile : (t + 1) * tile, span], preferred_element_type=jnp.float32
                 )
-            gated = (piece * gate_ref[:used, :]).astype(jnp.bfloat16)
+            gated = (piece * gate).astype(jnp.bfloat16)
             for i, block in enumerate(blocks):
-                term = jnp.dot(back_ref[i], gated[i * capacity : (i + 1) * capacity], preferred_element_type=jnp.float32)
-                term_ref[block, :, span] = term.astype(jnp.bfloat16)
+                term_ref[block, :, span] = gated[i * rows : (i + 1) * rows]
 
     pl.semaphore_wait(barrier, len(peers))
     for j in parts:
@@ -497,11 +481,9 @@
             if half > 1 or last(index, j):
                 hop(index, way, 0, j).start()
         relay(0, 0, j).start()
-    for copy in loads:
-        copy.wait()
     for j in parts:
         relay(0, 0, j).wait_recv()
-    compute([0], [])
+    compute([0], [], fresh=True)
     share(0, 0).start()
     for j in parts:
         forward(1, j)
@@ -527,14 +509,7 @@
     ready(half - 1)
     compute([1 - half, half - 1], [functools.partial(forward, half, j) for j in parts])
     pair_up(half - 1)
-    for j in parts:
-        for index, way in ways:
-            if last(index, j):
-                relay(index * half + half, -way * half, j).wait_recv()
-    compute([half], [])
-    share(half, half).start()
-
-    arrived, hops = set(), {}
+    arrived = set()
 
     def slot_of(offset):
         return offset + half if 0 < offset < half else abs(offset)
@@ -547,34 +522,50 @@
         mine = term_ref[ring.block(offset, ring.core), chunk, :].astype(jnp.float32)
         return mine + got[slot_of(offset), chunk, :].astype(jnp.float32)
 
-    for step in range(half):
+    def travelling(index, way, step, j):
+        return remote(
+            outgoing.at[index, step, chunks[j]],
+            incoming.at[index, step, chunks[j]],
+            ring_send.at[index, step, j],
+            ring_recv.at[index, step, j],
+            ring.device(way),
+        )
+
+    def ring_step(step, final):
         for j, chunk in enumerate(chunks):
             for index, way in ways:
-                if step == 0 and not last(index, j):
+                if last(index, j) != final:
                     continue
                 total = pair(way * (half - step), chunk)
-                if (index, step - 1, j) in hops:
-                    hops[index, step - 1, j].wait_recv()
+                if step > (0 if final else 1):
+                    travelling(index, way, step - 1, j).wait_recv()
                     total = total + incoming[index, step - 1, chunk, :].astype(jnp.float32)
                 outgoing[index, step, chunk, :] = total.astype(jnp.bfloat16)
-                hops[index, step, j] = remote(
-                    outgoing.at[index, step, chunk],
-                    incoming.at[index, step, chunk],
-                    ring_send.at[index, step, j],
-                    ring_recv.at[index, step, j],
-                    ring.device(way),
-                )
-                hops[index, step, j].start()
+                travelling(index, way, step, j).start()
+
+    ring_step(1, False)
+    for j in parts:
+        for index, way in ways:
+            if last(index, j):
+                relay(index * half + half, -way * half, j).wait_recv()
+    compute([half], [lambda: None, lambda: None, functools.partial(ring_step, 2, False)])
+    share(half, half).start()
+
+    for step in range(half):
+        ring_step(step, True)
+        if step + 3 < half:
+            ring_step(step + 3, False)
     for j, chunk in enumerate(chunks):
         total = pair(0, chunk) + residual_ref[chunk, :].astype(jnp.float32)
-        for index in (0, 1):
-            if (index, half - 1, j) in hops:
-                hops[index, half - 1, j].wait_recv()
-                total = total + incoming[index, half - 1, chunk, :].astype(jnp.float32)
+        for index, way in ways:
+            travelling(index, way, half - 1, j).wait_recv()
+            total = total + incoming[index, half - 1, chunk, :].astype(jnp.float32)
         out_ref[chunk, :] = total.astype(jnp.bfloat16)
 
-    for copy in hops.values():
-        copy.wait_send()
+    for j in parts:
+        for index, way in ways:
+            for step in range(0 if last(index, j) else 1, half):
+                travelling(index, way, step, j).wait_send()
     share(0, 0).wait_send()
     share(half, half).wait_send()
     for j in parts:
@@ -600,7 +591,7 @@
     lax.fori_loop(1, half, drain, 0)
 
 
-def norm_and_experts(residual, norm_gain, router, routes, w_gate_up, w_down, capacity):
+def norm_and_experts(residual, norm_gain, router, routes, w_gate_up, w_down):
     chips, heads = lax.axis_size("ctx") // CORES, lax.axis_size("head")
     rows, width = residual.shape
     tokens = rows * heads
@@ -610,14 +601,13 @@
     half = chips * heads // 2
     blocks = chips * heads * CORES
     parts = len(row_chunks(rows))
-    capacity = -(-capacity // 16) * 16
     tile = hidden_units // 3 if hidden_units % 48 == 0 else hidden_units
     columns = 8 * LANES
     most = 2 * CORES
     bf16, f32, dma = jnp.bfloat16, jnp.float32, pltpu.SemaphoreType.DMA
     anywhere = pl.BlockSpec(memory_space=pl.ANY)
     return pl.pallas_call(
-        functools.partial(layer_kernel, chips, heads, experts, capacity, tile, columns),
+        functools.partial(layer_kernel, chips, heads, experts, tile, columns),
         out_shape=jax.ShapeDtypeStruct((rows, width), bf16),
         in_specs=[full_vmem()] * 4 + [anywhere] * 2,
         out_specs=full_vmem(),
@@ -627,15 +617,12 @@
             pltpu.VMEM((LANES, width), bf16),
             pltpu.VMEM((2, hidden_units, width), bf16),
             pltpu.VMEM((hidden_units, width), bf16),
-            pltpu.VMEM((most * capacity, width), bf16),
-            pltpu.VMEM((hidden_units // tile, most * capacity, tile), bf16),
-            pltpu.VMEM((most * capacity, 1), f32),
-            pltpu.VMEM((most, rows, capacity), bf16),
+            pltpu.VMEM((hidden_units // tile, most * rows, tile), bf16),
             pltpu.VMEM((blocks, rows, width), bf16),
             pltpu.VMEM((2 * half, rows, width), bf16),
             pltpu.VMEM((2, half, rows, width), bf16),
             pltpu.VMEM((2, half, rows, width), bf16),
-            dma((2,)),
+            dma((3, hidden_units // tile)),
             dma((2, half, parts)),
             dma((2, half, parts)),
             dma((2 * half + 1, parts)),
@@ -651,7 +638,7 @@
         name="norm_and_experts",
     )(
         residual,
-        norm_gain.reshape(1, -1),
+        norm_gain,
         router.T,
         routes.T,
         jnp.swapaxes(w_gate_up[0], 1, 2),
@@ -673,13 +660,8 @@
     w_gate_up,
     w_down,
 ):
-    n_ctx = lax.axis_size("ctx")
-    n_head = lax.axis_size("head")
-    tok_count = queries.shape[0]
-    top_count = routes.shape[1]
-    capacity = max(2, min(tok_count // n_head, 3 * tok_count * top_count // (2 * n_head * n_ctx)))
     residual = attend(queries, keys, values, sinks, segments, hidden_in, w_out)
-    return norm_and_experts(residual, norm_gain, router, routes, w_gate_up, w_down, capacity)
+    return norm_and_experts(residual, norm_gain, router, routes, w_gate_up, w_down)
 
 
 def solution(mesh):

time: 134 us -> 123 us (0.918)
  Pallas kernels: 130 us -> 121 us
    pallas_call x1, Pallas kernels: 101 us -> 91.2 us  [norm_and_experts(): pl.pallas_call(functools.partial(layer_kernel, chips, heads, experts, til...]
where the time goes in v2:
time: 123 us
  Pallas kernels  121 us (98%)
  local copies, waits for them, and re-layouts  1.76 us (1%)
    pallas_call x1, Pallas kernels, norm_and_experts(): pl.pallas_call(functools.partial(layer_kernel, chips, heads, experts, til...  91.2 us
    pallas_call x1, Pallas kernels, attend(): pl.pallas_call(functools.partial(attend_kernel, chips, heads), out_shape=...  29.8 us

profile of v2, /device:TPU:0, one launch (start us, length us, event | category | flops | bytes accessed | tf_op | source)
XLA Modules:
  0.0 122.7 jit_solution(4079641803324013028)
XLA Ops:
  0.0 29.8 %attend.1.residual_ref = bf16[64,2880]{1,0:T(8,128)(2,1)} custom-call(bf16[128,256]{1,0:T(8,128)(2,1)} %key_ref.1, bf16[128,256]{1,0:T(8,128)(2,1)} %value_ref.1, bf16[128,2048]{1,0:T(8,128)(2,1)} %query_ref.1, f32[32]{0:T(128)} %sink_ref.1, s32[1,1024]{1,0:T(1,128)} %bitcast.14, bf16[2880,128]{1,0:T(8,128)(2,1)} %bitcast.12, bf16[2880,2048]{1,0:T(8,128)(2,1)} %bitcast.10), custom_call_target="tpu_custom_call" | custom-call | tf_op jit(solution)/shard_map/attend/pallas_call | solution.py:292
  29.8 91.2 %norm_and_experts.1 = bf16[64,2880]{1,0:T(8,128)(2,1)} custom-call(bf16[64,2880]{1,0:T(8,128)(2,1)} %attend.1.residual_ref, f32[2880]{0:T(1024)} %gain_ref.1, bf16[8,2880]{1,0:T(8,128)(2,1)} %bitcast.13, s32[4,128]{1,0:T(4,128)} %bitcast.15, bf16[2,1440,2880]{2,1,0:T(8,128)(2,1)} %bitcast.9, bf16[1440,2880]{1,0:T(8,128)(2,1)} %bitcast.11), custom_call_target="tpu_custom_call" | custom-call | tf_op jit(solution)/shard_map/norm_and_experts/pallas_call | solution.py:609
  121.0 1.8 %copy.14 = bf16[64,2880]{1,0:T(8,128)(2,1)} copy(bf16[64,2880]{1,0:T(8,128)(2,1)} %norm_and_experts.1) | data formatting | bytes 737280

commit v3 on v2

--- a/solution.py
+++ b/solution.py
@@ -54,10 +54,9 @@
     )
 
 
-def row_chunks(rows):
-    if rows % 32 == 0:
-        return [pl.ds(0, rows // 2), pl.ds(rows // 2, rows // 2)]
-    return [pl.ds(0, rows)]
+def row_chunks(rows, most):
+    count = most if rows % (16 * most) == 0 else 1
+    return [pl.ds(first, rows // count) for first in range(0, rows, rows // count)]
 
 
 def attend_kernel(
@@ -228,7 +227,7 @@
         attended_ref[:, span] = jnp.concatenate(both, axis=1)
         return carry
 
-    lax.fori_loop(0, groups * share // 2, mix, 0)
+    lax.fori_loop(0, groups * share // 2, mix, 0, unroll=2)
 
     load.wait()
     spans = column_spans(part_ref.shape[1])
@@ -327,7 +326,7 @@
 
 
 def layer_kernel(
-    chips, heads, experts, tile, columns, residual_ref, gain_ref, router_ref, route_ref, up_hbm, down_hbm,
+    chips, heads, experts, tile, columns, most, residual_ref, gain_ref, router_ref, route_ref, up_hbm, down_hbm,
     out_ref, all_ref, route_rows, lanes_ref, up_ref, down_ref, act_ref, term_ref, got, outgoing, incoming, weight_sem,
     hop_send, hop_recv, copy_send, copy_recv, pair_send, pair_recv, ring_send, ring_recv,
 ):
@@ -335,8 +334,10 @@
     count, half = ring.count, ring.count // 2
     rows, width = out_ref.shape
     start = width % LANES
-    chunks = row_chunks(rows)
+    chunks, bits = row_chunks(rows, 2), row_chunks(rows, 4)
     parts = range(len(chunks))
+    depth = len(bits) // len(chunks)
+    order = [part * depth + j for j in range(depth) for part in parts]
     ways = ((0, 1), (1, -1))
     turned = (((1,), (1,)), ((), ()))
     ctx, head = lax.axis_index("ctx"), ring.head
@@ -410,30 +411,27 @@
         view = all_ref.at[ring.block(offset, ring.core), chunks[j]]
         return remote(view, view, copy_send.at[slot, j], copy_recv.at[slot, j], ring.partner)
 
+    def continues(index, step, j):
+        return step < half - 1 or (step == half - 1 and last(index, j))
+
     def forward(step, j):
         for index, way in ways:
-            if isinstance(step, int) and step == half and not last(index, j):
-                continue
-            hop(index, way, step - 1, j).wait_recv()
-            if last(index, j):
-                if not (isinstance(step, int) and step == half):
+            if continues(index, step - 1, j):
+                hop(index, way, step - 1, j).wait_recv()
+                if continues(index, step, j):
                     hop(index, way, step, j).start()
-            elif not isinstance(step, int):
-
-                @pl.when(step < half - 1)
-                def _():
-                    hop(index, way, step, j).start()
-
-            elif step < half - 1:
-                hop(index, way, step, j).start()
-            relay(index * half + step, -way * step, j).start()
-
-    def share(slot, offset):
+                relay(index * half + step, -way * step, j).start()
+
+    def slot_of(offset):
+        return offset + half if 0 < offset < half else abs(offset)
+
+    def share(offset):
+        slot = slot_of(offset)
         return remote(
             term_ref.at[ring.block(offset, 1 - ring.core)], got.at[slot], pair_send.at[slot], pair_recv.at[slot], ring.partner
         )
 
-    def compute(offsets, hooks, fresh=False):
+    def multiply_blocks(offsets, hooks, fresh):
         blocks = [ring.block(offset, core) for offset in offsets for core in range(CORES)]
         used = len(blocks) * rows
         gates = []
@@ -453,11 +451,13 @@
             a = lax.dot_general(x, up_ref[0, span, :], turned, preferred_element_type=jnp.float32)
             b = lax.dot_general(x, up_ref[1, span, :], turned, preferred_element_type=jnp.float32)
             act_ref[t, :used, :] = (a * jax.nn.sigmoid(1.702 * a) * (b + 1.0)).astype(jnp.bfloat16)
-            for spot, hook in enumerate(hooks):
-
-                @pl.when(t == min(spot, tiles - 1))
-                def _():
-                    hook()
+            for spot in range(3):
+                if hooks[spot]:
+
+                    @pl.when(t == min(spot, tiles - 1))
+                    def _():
+                        for hook in hooks[spot]:
+                            hook()
 
             return carry
 
@@ -474,121 +474,120 @@
             gated = (piece * gate).astype(jnp.bfloat16)
             for i, block in enumerate(blocks):
                 term_ref[block, :, span] = gated[i * rows : (i + 1) * rows]
+            if first == columns:
+                for hook in hooks[3]:
+                    hook()
+
+    def experts_on(offsets, hooks=((), (), (), ()), fresh=False):
+        for offset in offsets:
+            for index, way in ways:
+                for j in parts:
+                    distance = abs(offset)
+                    if offset == 0:
+                        if index == 0:
+                            relay(0, 0, j).wait_recv()
+                    elif continues(index, distance - 1, j) and (distance == half or offset == -way * distance):
+                        relay(index * half + distance, -way * distance, j).wait_recv()
+        for first in range(0, len(offsets), most):
+            multiply_blocks(offsets[first : first + most], hooks, fresh)
+            hooks, fresh = ((), (), (), ()), False
+        for offset in offsets:
+            share(offset).start()
+
+    arrived = set()
+
+    def pair(offset, bit):
+        offset = half if offset == -half else offset
+        if offset not in arrived:
+            share(offset).wait_recv()
+            arrived.add(offset)
+        mine = term_ref[ring.block(offset, ring.core), bits[bit], :].astype(jnp.float32)
+        return mine + got[slot_of(offset), bits[bit], :].astype(jnp.float32)
+
+    def travelling(index, way, step, bit):
+        return remote(
+            outgoing.at[index, step, bits[bit]],
+            incoming.at[index, step, bits[bit]],
+            ring_send.at[index, step, bit],
+            ring_recv.at[index, step, bit],
+            ring.device(way),
+        )
+
+    def ring_step(final, step, bit):
+        for index, way in ways:
+            if last(index, bit // depth) == final:
+                total = pair(way * (half - step), bit)
+                if step > (0 if final else 1):
+                    travelling(index, way, step - 1, bit).wait_recv()
+                    total = total + incoming[index, step - 1, bits[bit], :].astype(jnp.float32)
+                outgoing[index, step, bits[bit], :] = total.astype(jnp.bfloat16)
+                travelling(index, way, step, bit).start()
+
+    def finish(bit):
+        total = pair(0, bit) + residual_ref[bits[bit], :].astype(jnp.float32)
+        for index, way in ways:
+            travelling(index, way, half - 1, bit).wait_recv()
+            total = total + incoming[index, half - 1, bits[bit], :].astype(jnp.float32)
+        out_ref[bits[bit], :] = total.astype(jnp.bfloat16)
+
+    def gather(step, j):
+        return functools.partial(forward, step, j)
+
+    def short(step, bit):
+        return functools.partial(ring_step, False, step, bit)
 
     pl.semaphore_wait(barrier, len(peers))
     for j in parts:
         for index, way in ways:
-            if half > 1 or last(index, j):
+            if continues(index, 0, j):
                 hop(index, way, 0, j).start()
         relay(0, 0, j).start()
-    for j in parts:
-        relay(0, 0, j).wait_recv()
-    compute([0], [], fresh=True)
-    share(0, 0).start()
-    for j in parts:
-        forward(1, j)
-
-    def ready(distance):
-        for index, way in ways:
+    if depth == 2 and half == 4:
+        experts_on([0], ((), (), [gather(1, 0)], ()), fresh=True)
+        forward(1, 1)
+        experts_on([1, -1], ((), [gather(2, 0)], (), ()))
+        forward(2, 1)
+        experts_on([2, -2], ((), [gather(3, 0)], (), [gather(3, 1)]))
+        experts_on([3, -3], ((), [gather(4, 0), gather(4, 1)], (), ()))
+        for bit in order:
+            ring_step(False, 1, bit)
+        experts_on([4], ((), (), [short(2, 0), short(2, 2)], [short(2, 1), short(2, 3)]))
+        for bit in order:
+            ring_step(True, 0, bit)
+        for bit in order:
+            ring_step(False, 3, bit)
+        for step in (1, 2, 3):
+            for bit in order:
+                ring_step(True, step, bit)
+    else:
+        for step in range(1, half + 1):
             for j in parts:
-                relay(index * half + distance, -way * distance, j).wait_recv()
-
-    def pair_up(distance):
-        for index, way in ways:
-            share(index * half + distance, -way * distance).start()
-
-    def travel(distance, carry):
-        ready(distance)
-        compute(
-            [-way * distance for index, way in ways], [functools.partial(forward, distance + 1, j) for j in parts]
-        )
-        pair_up(distance)
-        return carry
-
-    lax.fori_loop(1, half - 1, travel, 0)
-    ready(half - 1)
-    compute([1 - half, half - 1], [functools.partial(forward, half, j) for j in parts])
-    pair_up(half - 1)
-    arrived = set()
-
-    def slot_of(offset):
-        return offset + half if 0 < offset < half else abs(offset)
-
-    def pair(offset, chunk):
-        offset = half if offset == -half else offset
-        if offset not in arrived:
-            share(slot_of(offset), offset).wait_recv()
-            arrived.add(offset)
-        mine = term_ref[ring.block(offset, ring.core), chunk, :].astype(jnp.float32)
-        return mine + got[slot_of(offset), chunk, :].astype(jnp.float32)
-
-    def travelling(index, way, step, j):
-        return remote(
-            outgoing.at[index, step, chunks[j]],
-            incoming.at[index, step, chunks[j]],
-            ring_send.at[index, step, j],
-            ring_recv.at[index, step, j],
-            ring.device(way),
-        )
-
-    def ring_step(step, final):
-        for j, chunk in enumerate(chunks):
-            for index, way in ways:
-                if last(index, j) != final:
-                    continue
-                total = pair(way * (half - step), chunk)
-                if step > (0 if final else 1):
-                    travelling(index, way, step - 1, j).wait_recv()
-                    total = total + incoming[index, step - 1, chunk, :].astype(jnp.float32)
-                outgoing[index, step, chunk, :] = total.astype(jnp.bfloat16)
-                travelling(index, way, step, j).start()
-
-    ring_step(1, False)
-    for j in parts:
-        for index, way in ways:
-            if last(index, j):
-                relay(index * half + half, -way * half, j).wait_recv()
-    compute([half], [lambda: None, lambda: None, functools.partial(ring_step, 2, False)])
-    share(half, half).start()
-
-    for step in range(half):
-        ring_step(step, True)
-        if step + 3 < half:
-            ring_step(step + 3, False)
-    for j, chunk in enumerate(chunks):
-        total = pair(0, chunk) + residual_ref[chunk, :].astype(jnp.float32)
-        for index, way in ways:
-            travelling(index, way, half - 1, j).wait_recv()
-            total = total + incoming[index, half - 1, chunk, :].astype(jnp.float32)
-        out_ref[chunk, :] = total.astype(jnp.bfloat16)
-
-    for j in parts:
-        for index, way in ways:
-            for step in range(0 if last(index, j) else 1, half):
-                travelling(index, way, step, j).wait_send()
-    share(0, 0).wait_send()
-    share(half, half).wait_send()
+                forward(step, j)
+        offsets = [0]
+        for distance in range(1, half):
+            offsets += [distance, -distance]
+        experts_on(offsets + [half], fresh=True)
+        for step in range(half):
+            for bit in order:
+                ring_step(True, step, bit)
+                if step > 0:
+                    ring_step(False, step, bit)
+    for bit in order:
+        finish(bit)
+
+    for offset in range(1 - half, half + 1):
+        share(offset).wait_send()
     for j in parts:
         relay(0, 0, j).wait_send()
-        for index, way in ways:
-            if last(index, j):
-                hop(index, way, half - 1, j).wait_send()
-                relay(index * half + half, -way * half, j).wait_send()
-            hop(index, way, 0, j).wait_send()
-
-    def drain(step, carry):
-        for index, way in ways:
-            share(index * half + step, -way * step).wait_send()
+    for index, way in ways:
+        for step in range(half):
             for j in parts:
-                relay(index * half + step, -way * step, j).wait_send()
-
-                @pl.when(step < half - 1)
-                def _():
+                if continues(index, step, j):
                     hop(index, way, step, j).wait_send()
-
-        return carry
-
-    lax.fori_loop(1, half, drain, 0)
+                    relay(index * half + step + 1, -way * (step + 1), j).wait_send()
+            for bit in order:
+                if step > 0 or last(index, bit // depth):
+                    travelling(index, way, step, bit).wait_send()
 
 
 def norm_and_experts(residual, norm_gain, router, routes, w_gate_up, w_down):
@@ -600,14 +599,14 @@
     padded = width - width % LANES + LANES
     half = chips * heads // 2
     blocks = chips * heads * CORES
-    parts = len(row_chunks(rows))
+    parts, bits = len(row_chunks(rows, 2)), len(row_chunks(rows, 4))
     tile = hidden_units // 3 if hidden_units % 48 == 0 else hidden_units
     columns = 8 * LANES
-    most = 2 * CORES
+    most = 2
     bf16, f32, dma = jnp.bfloat16, jnp.float32, pltpu.SemaphoreType.DMA
     anywhere = pl.BlockSpec(memory_space=pl.ANY)
     return pl.pallas_call(
-        functools.partial(layer_kernel, chips, heads, experts, tile, columns),
+        functools.partial(layer_kernel, chips, heads, experts, tile, columns, most),
         out_shape=jax.ShapeDtypeStruct((rows, width), bf16),
         in_specs=[full_vmem()] * 4 + [anywhere] * 2,
         out_specs=full_vmem(),
@@ -617,7 +616,7 @@
             pltpu.VMEM((LANES, width), bf16),
             pltpu.VMEM((2, hidden_units, width), bf16),
             pltpu.VMEM((hidden_units, width), bf16),
-            pltpu.VMEM((hidden_units // tile, most * rows, tile), bf16),
+            pltpu.VMEM((hidden_units // tile, most * CORES * rows, tile), bf16),
             pltpu.VMEM((blocks, rows, width), bf16),
             pltpu.VMEM((2 * half, rows, width), bf16),
             pltpu.VMEM((2, half, rows, width), bf16),
@@ -629,8 +628,8 @@
             dma((2 * half + 1, parts)),
             dma((2 * half,)),
             dma((2 * half,)),
-            dma((2, half, parts)),
-            dma((2, half, parts)),
+            dma((2, half, bits)),
+            dma((2, half, bits)),
         ],
         compiler_params=pltpu.CompilerParams(
             collective_id=1, has_side_effects=True, vmem_limit_bytes=60 * 1024 * 1024

time: 123 us -> 117 us (0.951)
  Pallas kernels: 121 us -> 115 us
    pallas_call x1, Pallas kernels: 91.2 us -> 87.8 us  [norm_and_experts(): pl.pallas_call(functools.partial(layer_kernel, chips, heads, experts, til...]
    pallas_call x1, Pallas kernels: 29.8 us -> 27 us  [attend(): pl.pallas_call(functools.partial(attend_kernel, chips, heads), out_shape=...]
where the time goes in v3:
time: 117 us
  Pallas kernels  115 us (98%)
  local copies, waits for them, and re-layouts  1.76 us (2%)
    pallas_call x1, Pallas kernels, norm_and_experts(): pl.pallas_call(functools.partial(layer_kernel, chips, heads, experts, til...  87.8 us
    pallas_call x1, Pallas kernels, attend(): pl.pallas_call(functools.partial(attend_kernel, chips, heads), out_shape=...  27 us

profile of v3, /device:TPU:0, one launch (start us, length us, event | category | flops | bytes accessed | tf_op | source)
XLA Modules:
  0.0 116.5 jit_solution(13300742120770831972)
XLA Ops:
  0.0 27.0 %attend.1.residual_ref = bf16[64,2880]{1,0:T(8,128)(2,1)} custom-call(bf16[128,256]{1,0:T(8,128)(2,1)} %key_ref.1, bf16[128,256]{1,0:T(8,128)(2,1)} %value_ref.1, bf16[128,2048]{1,0:T(8,128)(2,1)} %query_ref.1, f32[32]{0:T(128)} %sink_ref.1, s32[1,1024]{1,0:T(1,128)} %bitcast.14, bf16[2880,128]{1,0:T(8,128)(2,1)} %bitcast.12, bf16[2880,2048]{1,0:T(8,128)(2,1)} %bitcast.10), custom_call_target="tpu_custom_call" | custom-call | tf_op jit(solution)/shard_map/attend/pallas_call | solution.py:291
  27.0 87.8 %norm_and_experts.1 = bf16[64,2880]{1,0:T(8,128)(2,1)} custom-call(bf16[64,2880]{1,0:T(8,128)(2,1)} %attend.1.residual_ref, f32[2880]{0:T(1024)} %gain_ref.1, bf16[8,2880]{1,0:T(8,128)(2,1)} %bitcast.13, s32[4,128]{1,0:T(4,128)} %bitcast.15, bf16[2,1440,2880]{2,1,0:T(8,128)(2,1)} %bitcast.9, bf16[1440,2880]{1,0:T(8,128)(2,1)} %bitcast.11), custom_call_target="tpu_custom_call" | custom-call | tf_op jit(solution)/shard_map/norm_and_experts/pallas_call | solution.py:608
  114.8 1.8 %copy.14 = bf16[64,2880]{1,0:T(8,128)(2,1)} copy(bf16[64,2880]{1,0:T(8,128)(2,1)} %norm_and_experts.1) | data formatting | bytes 737280

commit v4 on v3

--- a/solution.py
+++ b/solution.py
@@ -151,7 +151,7 @@
             peak_ref[span] = peak if step == 0 else jnp.maximum(peak_ref[span], peak)
             return carry
 
-        lax.fori_loop(0, groups, one, 0)
+        lax.fori_loop(0, groups, one, 0, unroll=2)
 
     def take_values(step):
         relay(step, 1).wait_recv()
@@ -161,6 +161,7 @@
                 :, group * HEAD_SIZE : (group + 1) * HEAD_SIZE
             ]
 
+    hidden_rows[...] = hidden_ref[...].T
     relay(0, 0).wait_recv()
     score(0)
     for step in range(1, chips):
@@ -197,7 +198,6 @@
         take_values(chips - 1)
 
     own = pl.ds(pl.multiple_of(head * own_rows, own_rows), own_rows)
-    hidden_rows[...] = hidden_ref[...].T
 
     def mix(couple, carry):
         group = lax.div(couple * 2, share)
@@ -227,7 +227,7 @@
         attended_ref[:, span] = jnp.concatenate(both, axis=1)
         return carry
 
-    lax.fori_loop(0, groups * share // 2, mix, 0, unroll=2)
+    lax.fori_loop(0, groups * share // 2, mix, 0, unroll=4)
 
     load.wait()
     spans = column_spans(part_ref.shape[1])
@@ -273,7 +273,7 @@
 
 
 def column_spans(padded):
-    wide = 8 * LANES
+    wide = 4 * LANES
     return [(first, min(wide, padded - first)) for first in range(0, padded, wide)]
 
 
@@ -545,8 +545,7 @@
     if depth == 2 and half == 4:
         experts_on([0], ((), (), [gather(1, 0)], ()), fresh=True)
         forward(1, 1)
-        experts_on([1, -1], ((), [gather(2, 0)], (), ()))
-        forward(2, 1)
+        experts_on([1, -1], ((), [gather(2, 0)], (), [gather(2, 1)]))
         experts_on([2, -2], ((), [gather(3, 0)], (), [gather(3, 1)]))
         experts_on([3, -3], ((), [gather(4, 0), gather(4, 1)], (), ()))
         for bit in order:

time: 117 us -> 112 us (0.957)
  Pallas kernels: 115 us -> 110 us
    pallas_call x1, Pallas kernels: 27 us -> 24.6 us  [attend(): pl.pallas_call(functools.partial(attend_kernel, chips, heads), out_shape=...]
    pallas_call x1, Pallas kernels: 87.8 us -> 85.8 us  [norm_and_experts(): pl.pallas_call(functools.partial(layer_kernel, chips, heads, experts, til...]
where the time goes in v4:
time: 112 us
  Pallas kernels  110 us (98%)
  local copies, waits for them, and re-layouts  1.76 us (2%)
    pallas_call x1, Pallas kernels, norm_and_experts(): pl.pallas_call(functools.partial(layer_kernel, chips, heads, experts, til...  85.8 us
    pallas_call x1, Pallas kernels, attend(): pl.pallas_call(functools.partial(attend_kernel, chips, heads), out_shape=...  24.6 us

profile of v4, /device:TPU:0, one launch (start us, length us, event | category | flops | bytes accessed | tf_op | source)
XLA Modules:
  0.0 112.2 jit_solution(3874237284447597366)
XLA Ops:
  0.0 24.6 %attend.1.residual_ref = bf16[64,2880]{1,0:T(8,128)(2,1)} custom-call(bf16[128,256]{1,0:T(8,128)(2,1)} %key_ref.1, bf16[128,256]{1,0:T(8,128)(2,1)} %value_ref.1, bf16[128,2048]{1,0:T(8,128)(2,1)} %query_ref.1, f32[32]{0:T(128)} %sink_ref.1, s32[1,1024]{1,0:T(1,128)} %bitcast.14, bf16[2880,128]{1,0:T(8,128)(2,1)} %bitcast.12, bf16[2880,2048]{1,0:T(8,128)(2,1)} %bitcast.10), custom_call_target="tpu_custom_call" | custom-call | tf_op jit(solution)/shard_map/attend/pallas_call | solution.py:291
  24.6 85.8 %norm_and_experts.1 = bf16[64,2880]{1,0:T(8,128)(2,1)} custom-call(bf16[64,2880]{1,0:T(8,128)(2,1)} %attend.1.residual_ref, f32[2880]{0:T(1024)} %gain_ref.1, bf16[8,2880]{1,0:T(8,128)(2,1)} %bitcast.13, s32[4,128]{1,0:T(4,128)} %bitcast.15, bf16[2,1440,2880]{2,1,0:T(8,128)(2,1)} %bitcast.9, bf16[1440,2880]{1,0:T(8,128)(2,1)} %bitcast.11), custom_call_target="tpu_custom_call" | custom-call | tf_op jit(solution)/shard_map/norm_and_experts/pallas_call | solution.py:607
  110.5 1.8 %copy.14 = bf16[64,2880]{1,0:T(8,128)(2,1)} copy(bf16[64,2880]{1,0:T(8,128)(2,1)} %norm_and_experts.1) | data formatting | bytes 737280

commit v5 on v4

--- a/solution.py
+++ b/solution.py
@@ -227,7 +227,7 @@
         attended_ref[:, span] = jnp.concatenate(both, axis=1)
         return carry
 
-    lax.fori_loop(0, groups * share // 2, mix, 0, unroll=4)
+    lax.fori_loop(0, groups * share // 2, mix, 0, unroll=min(8, groups * share // 2))
 
     load.wait()
     spans = column_spans(part_ref.shape[1])
@@ -273,7 +273,7 @@
 
 
 def column_spans(padded):
-    wide = 4 * LANES
+    wide = 2 * LANES
     return [(first, min(wide, padded - first)) for first in range(0, padded, wide)]
 
 
@@ -550,7 +550,7 @@
         experts_on([3, -3], ((), [gather(4, 0), gather(4, 1)], (), ()))
         for bit in order:
             ring_step(False, 1, bit)
-        experts_on([4], ((), (), [short(2, 0), short(2, 2)], [short(2, 1), short(2, 3)]))
+        experts_on([4], ((), [short(2, 0), short(2, 2)], [short(2, 1), short(2, 3)], ()))
         for bit in order:
             ring_step(True, 0, bit)
         for bit in order:

time: 112 us -> 111 us (level)
  no operation moved by 1% of the time
where the time goes in v5:
time: 111 us
  Pallas kernels  109 us (98%)
  local copies, waits for them, and re-layouts  1.76 us (2%)
    pallas_call x1, Pallas kernels, norm_and_experts(): pl.pallas_call(functools.partial(layer_kernel, chips, heads, experts, til...  85.6 us
    pallas_call x1, Pallas kernels, attend(): pl.pallas_call(functools.partial(attend_kernel, chips, heads), out_shape=...  23.8 us

profile of v5, /device:TPU:0, one launch (start us, length us, event | category | flops | bytes accessed | tf_op | source)
XLA Modules:
  0.0 111.2 jit_solution(15330568378614201431)
XLA Ops:
  0.0 23.8 %attend.1.residual_ref = bf16[64,2880]{1,0:T(8,128)(2,1)} custom-call(bf16[128,256]{1,0:T(8,128)(2,1)} %key_ref.1, bf16[128,256]{1,0:T(8,128)(2,1)} %value_ref.1, bf16[128,2048]{1,0:T(8,128)(2,1)} %query_ref.1, f32[32]{0:T(128)} %sink_ref.1, s32[1,1024]{1,0:T(1,128)} %bitcast.14, bf16[2880,128]{1,0:T(8,128)(2,1)} %bitcast.12, bf16[2880,2048]{1,0:T(8,128)(2,1)} %bitcast.10), custom_call_target="tpu_custom_call" | custom-call | tf_op jit(solution)/shard_map/attend/pallas_call | solution.py:291
  23.8 85.6 %norm_and_experts.1 = bf16[64,2880]{1,0:T(8,128)(2,1)} custom-call(bf16[64,2880]{1,0:T(8,128)(2,1)} %attend.1.residual_ref, f32[2880]{0:T(1024)} %gain_ref.1, bf16[8,2880]{1,0:T(8,128)(2,1)} %bitcast.13, s32[4,128]{1,0:T(4,128)} %bitcast.15, bf16[2,1440,2880]{2,1,0:T(8,128)(2,1)} %bitcast.9, bf16[1440,2880]{1,0:T(8,128)(2,1)} %bitcast.11), custom_call_target="tpu_custom_call" | custom-call | tf_op jit(solution)/shard_map/norm_and_experts/pallas_call | solution.py:607
  109.4 1.8 %copy.14 = bf16[64,2880]{1,0:T(8,128)(2,1)} copy(bf16[64,2880]{1,0:T(8,128)(2,1)} %norm_and_experts.1) | data formatting | bytes 737280
